TPU v7x, 32 devices: a whole 2x2x4 slice. The times are simulated.
32 devices in a mesh: groups: 2 (over x), context: 16 (over z, y, core).
Axes of the slice: x: 2, y: 2, z: 4, core: 2. Of those that a mesh axis runs over, the one named last changes fastest.
Arguments:
- q_store: bfloat16 [4096, 4096], P(('groups', 'context')), parts along dimension 0, may hold values from -6 to 6
- k_store: bfloat16 [4096, 4096], P(('groups', 'context')), parts along dimension 0, may hold values from -6 to 6
- v_store: bfloat16 [4096, 4096], P(('groups', 'context')), parts along dimension 0, may hold values from -6 to 6
- plan: int32 [32, 128], P(('groups', 'context')), parts along dimension 0, may hold values from 0 to 127, each once within a row
- doc_ids: int32 [4096], P(('groups', 'context')), parts along dimension 0, may hold values from 0 to 3, never falling along the last dimension, each value on 1 to 1024 neighbouring positions
- gain: float32 [4096], replicated, may hold values from 0.5 to 1.5
Outputs:
- out_store: bfloat16 [4096, 4096], P(('groups', 'context')), parts along dimension 0
There are 2 independent parts, one for each index of `groups`. A program takes and returns all parts, laid end to end along the dimension named above; an argument that names none is the same for every part. Nothing has to cross between parts.
Inputs may be any that keep to these rules, and one draw needn't show every extreme that they name: Each row of plan names every offset below 128 once. `doc_ids`: never falls along positions; each document holds 1 to 1024 positions.
All inputs are finite; a program needn't handle non-finite values.
Results may differ from a plain program's by a relative error of at most 0.005.
Values may be sent and summed in bfloat16 or wider, within the bound.
No kernel may reach another device: no remote copies, remote signals or barrier semaphores. Data moves between devices by JAX's collectives and lax.ppermute only.
A program may use at most 320 MiB of HBM per device.

v0:
```python
import functools

import jax
import jax.numpy as jnp
from jax import lax
from jax.experimental import pallas as pl
from jax.experimental.pallas import tpu as pltpu
from jax.sharding import PartitionSpec as P


HEAD_DIM = 128
SPAN = 128
AXIS = "context"


def entering(part, axis, combine, identity):
    place = lax.axis_index(axis)
    gathered = jax.tree.map(lambda a: lax.all_gather(a, axis), part)
    state = jax.tree.map(lambda a, e: jnp.zeros_like(a) + jnp.asarray(e, a.dtype), part, identity)

    def one(lap, state):
        return combine(
            state, jax.tree.map(lambda a: lax.dynamic_index_in_dim(a, lap, 0, False), gathered)
        )

    return lax.fori_loop(0, place, one, state)


def merge_states(earlier, later):
    early_state, early_doc = earlier
    late_state, late_doc = later
    keep_early = jnp.logical_or(early_doc == late_doc, late_doc < 0)
    merged = late_state + jnp.where(
        keep_early[:, None, None], early_state, jnp.zeros_like(early_state)
    )
    return (merged, jnp.where(late_doc < 0, early_doc, late_doc))


def at_home(q_store, k_store, v_store, plan, doc_ids, gain):
    token_count = q_store.shape[0]
    head_count = q_store.shape[1] // HEAD_DIM
    span_count = token_count // SPAN
    placed = plan.reshape(-1)
    inverse = (
        jnp.zeros((token_count,), jnp.int32)
        .at[placed]
        .set(jnp.arange(token_count, dtype=jnp.int32))
    )

    def settle(arrived):
        return jnp.take(arrived, inverse, axis=0).reshape(span_count, SPAN, head_count, HEAD_DIM)

    docs = doc_ids.reshape(span_count, SPAN)
    last_doc = docs[:, -1]
    query_rows, key_rows, value_rows = (
        lax.all_to_all(q_store, AXIS, split_axis=0, concat_axis=0, tiled=True),
        lax.all_to_all(k_store, AXIS, split_axis=0, concat_axis=0, tiled=True),
        lax.all_to_all(v_store, AXIS, split_axis=0, concat_axis=0, tiled=True),
    )
    keys_home = settle(key_rows)
    values_home = settle(value_rows)
    tail_mask = (docs == last_doc[:, None]).astype(jnp.bfloat16)
    span_states = jnp.einsum(
        "cshd,cshe->chde",
        keys_home * tail_mask[:, :, None, None],
        values_home,
        preferred_element_type=jnp.float32,
    )
    device_part = (span_states[0], last_doc)
    identity = (jnp.zeros_like(span_states[0]), jnp.full((1,), -1, jnp.int32))
    running = entering(device_part, AXIS, merge_states, identity)
    carry_states = running[0].astype(jnp.bfloat16)[None]
    queries = settle(query_rows)
    causal = jnp.arange(SPAN)[:, None] >= jnp.arange(SPAN)[None, :]
    allowed = jnp.logical_and(causal[None], docs[:, :, None] == docs[:, None, :])
    scores = jnp.einsum("cthd,cshd->chts", queries, keys_home, preferred_element_type=jnp.float32)
    weights = jnp.where(allowed[:, None], scores, 0.0).astype(jnp.bfloat16)
    inner = jnp.einsum("chts,cshe->cthe", weights, values_home, preferred_element_type=jnp.float32)
    match = (docs == running[1][:, None]).astype(jnp.bfloat16)
    carried = jnp.einsum(
        "cthd,chde->cthe",
        queries * match[:, :, None, None],
        carry_states,
        preferred_element_type=jnp.float32,
    )
    mixed = inner + carried
    scale = lax.rsqrt(jnp.mean(mixed * mixed, axis=-1, keepdims=True) + 1e-06)
    normed = (mixed * scale * gain.reshape(head_count, HEAD_DIM)).astype(jnp.bfloat16)
    normed = normed.reshape(token_count, head_count * HEAD_DIM)
    leaving = jnp.take(normed, placed, axis=0)
    return lax.all_to_all(leaving, AXIS, split_axis=0, concat_axis=0, tiled=True)


VMEM = pl.BlockSpec(memory_space=pltpu.VMEM)
ANY = pl.BlockSpec(memory_space=pl.ANY)
HBM = pl.BlockSpec(memory_space=pltpu.HBM)
ROOM = pltpu.CompilerParams(vmem_limit_bytes=24 << 20)
CHUNKS = (10, 6)


def slots(pairs):
    far = list(range(pairs - 1, pairs // 2 - 1, -1))
    near = [1, *range(pairs // 2 - 1, 1, -1)]
    return list(zip(far + near, near + far)) + [(0, 0)]


def place():
    me = lax.axis_index(AXIS)
    mine, side = lax.shift_right_logical(me, 1), jnp.bitwise_and(me, 1)
    return mine, side


def peers(pairs):
    mine, side = place()
    return [
        jnp.bitwise_xor(mine, jnp.where(side == 0, zero, one)) for zero, one in slots(pairs)
    ]


def start_all(copies):
    for copy in copies:
        copy.start()
    return copies


def wait_all(copies):
    for copy in copies:
        copy.wait()


def rows_of(pair, share):
    return pl.ds(pl.multiple_of(pair * share, share), share)


def pack_kernel(pairs, heads, first, count, plan_ref, doc_ref, q_ref, k_ref, v_ref, *rest):
    pieces = rest[:pairs]
    plans, docs, notes, sems, note_sems = rest[pairs:]
    share = SPAN // (2 * pairs)
    copies = []
    if first == 0:
        read = start_all(
            [
                pltpu.make_async_copy(plan_ref, plans, note_sems.at[pairs]),
                pltpu.make_async_copy(doc_ref, docs, note_sems.at[pairs + 1]),
            ]
        )
    tiles = count * heads
    for m, peer in enumerate(peers(pairs)):
        for a, ref in enumerate((q_ref, k_ref, v_ref)):
            room = pieces[m].at[pl.ds(a * tiles, tiles)]
            copy = pltpu.make_async_copy(
                ref.at[pl.ds(first, count), pl.ds(peer * heads, heads)],
                room.reshape(count, heads, share, HEAD_DIM),
                sems.at[m, a],
            )
            copies += start_all([copy])
    if first == 0:
        wait_all(read)
        lane = lax.broadcasted_iota(jnp.int32, (SPAN, SPAN), 1)
        other = lax.broadcasted_iota(jnp.int32, (SPAN, SPAN), 0)
        half, within = lane // (pairs * share), lane % (pairs * share)
        source = (within // share * 2 + half) * share + within % share
        order = jnp.where(other == source, 1.0, 0.0).astype(jnp.bfloat16)
        places = jnp.dot(
            jnp.broadcast_to(plans[...].astype(jnp.bfloat16), (share, SPAN)),
            order,
            preferred_element_type=jnp.float32,
        )
        hit = other.astype(jnp.float32) == places[0:1]
        docs_here = jnp.dot(
            jnp.broadcast_to(docs[...].astype(jnp.bfloat16), (share, SPAN)),
            jnp.where(hit, 1.0, 0.0).astype(jnp.bfloat16),
            preferred_element_type=jnp.float32,
        )
        row = lax.broadcasted_iota(jnp.int32, (share, SPAN), 0)
        notes[0] = jnp.where(row == 0, places, docs_here).astype(jnp.bfloat16)
        copies += start_all(
            [
                pltpu.make_async_copy(notes, pieces[m].at[pl.ds(3 * tiles, 1)], note_sems.at[m])
                for m in range(pairs)
            ]
        )
    wait_all(copies)


def pack(pairs, first, count, plan, docs, q, k, v):
    heads, share = q.shape[1] // pairs, q.shape[2]
    tiles = 3 * count * heads + (first == 0)
    shape = jax.ShapeDtypeStruct((tiles, share, HEAD_DIM), q.dtype)
    return pl.pallas_call(
        functools.partial(pack_kernel, pairs, heads, first, count),
        out_shape=[shape] * pairs,
        in_specs=[HBM] * 5,
        out_specs=[ANY] * pairs,
        scratch_shapes=[
            pltpu.VMEM((1, SPAN), jnp.int32),
            pltpu.VMEM((1, SPAN), jnp.int32),
            pltpu.VMEM((1, share, SPAN), q.dtype),
            pltpu.SemaphoreType.DMA((pairs, 3)),
            pltpu.SemaphoreType.DMA((pairs + 2,)),
        ],
        compiler_params=ROOM,
        name="pack",
    )(plan, docs, q, k, v)


def mark_kernel(x_ref, out_ref):
    pass


def mark(x):
    return pl.pallas_call(
        mark_kernel,
        out_shape=jax.ShapeDtypeStruct((8, SPAN), jnp.float32),
        in_specs=[ANY],
        out_specs=ANY,
        compiler_params=ROOM,
        name="mark",
    )(x)


def collect_kernel(pairs, share, start, marked, *rest):
    rest = rest[marked:]
    pieces = rest[:pairs]
    out_ref, sems = rest[pairs:]
    copies = [
        pltpu.make_async_copy(
            pieces[m].at[pl.ds(start, out_ref.shape[0])],
            out_ref.at[:, rows_of(peer, share), :],
            sems.at[m],
        )
        for m, peer in enumerate(peers(pairs))
    ]
    wait_all(start_all(copies))


def collect(pairs, start, stop, pieces, marked):
    _, share, width = pieces[0].shape
    return pl.pallas_call(
        functools.partial(collect_kernel, pairs, share, start, len(marked)),
        out_shape=jax.ShapeDtypeStruct((stop - start, pairs * share, width), pieces[0].dtype),
        in_specs=[ANY] * (pairs + len(marked)),
        out_specs=ANY,
        scratch_shapes=[pltpu.SemaphoreType.DMA((pairs,))],
        compiler_params=ROOM,
        name="collect",
    )(*marked, *pieces)


def attend_kernel(pairs, share, width, first, count, last, gain_ref, *rest):
    rest = list(rest)
    take = lambda k: [rest.pop(0) for _ in range(k)]
    given = take(3) if first else None
    queries, own, other = take(3)
    outs = take(pairs)
    kept = [] if last else take(3)
    state, mixed_rows, sems = rest
    half = pairs * share
    mine, side = place()
    heads = width // HEAD_DIM
    tiles = count * heads
    lower = side == 0
    if first:
        carry_doc = given[0][...]
        state[...] = given[1][...]
        lower_notes, upper_notes = given[2][:half], given[2][half:]
    else:
        carry_doc = jnp.full((1, SPAN), -1.0, jnp.float32)
        state[...] = jnp.zeros_like(state)
        lower_notes = jnp.where(lower, own[2 * tiles], other[2 * tiles])
        upper_notes = jnp.where(lower, other[2 * tiles], own[2 * tiles])
    if not last:
        kept[2][:half] = lower_notes
        kept[2][half:] = upper_notes
    gains = [gain_ref[pl.ds(mine * heads + h, 1), :] for h in range(heads)]

    def block(d, carry_doc):
        at = (first + d) // 2 * share
        said = (upper_notes if (first + d) % 2 else lower_notes)[at : at + share]
        said = said.astype(jnp.float32)
        said = jnp.where(lower, said, pltpu.roll(said, SPAN // 2, axis=1))
        place_s, doc_s = said[0:1], said[1:2]
        key_s = doc_s * SPAN + place_s
        key_t = jnp.transpose(jnp.broadcast_to(key_s, (SPAN, SPAN)))[:half]
        doc_t = jnp.floor(key_t * (1.0 / SPAN))
        allowed = jnp.logical_and(key_s <= key_t, key_s >= doc_t * SPAN)
        last_doc = jnp.broadcast_to(jnp.max(doc_s, axis=1, keepdims=True), (1, SPAN))
        match = doc_t == carry_doc
        tail = jnp.where(doc_s == last_doc, 1.0, 0.0).astype(jnp.bfloat16)
        keep = carry_doc == last_doc
        for h in range(heads):
            cols = slice(h * HEAD_DIM, (h + 1) * HEAD_DIM)
            tile = d * heads + h
            q = queries[tile]
            k, v = (
                jnp.concatenate([own[a * tiles + tile], other[a * tiles + tile]])
                for a in range(2)
            )
            turned = jnp.transpose(k)
            carry = state[h]
            scores = jnp.dot(q, turned, preferred_element_type=jnp.float32)
            carried = jnp.dot(q, carry.astype(jnp.bfloat16), preferred_element_type=jnp.float32)
            weights = jnp.where(allowed, scores, 0.0).astype(jnp.bfloat16)
            inner = jnp.dot(weights, v, preferred_element_type=jnp.float32)
            fresh = jnp.dot(turned * tail, v, preferred_element_type=jnp.float32)
            state[h] = fresh + jnp.where(keep, carry, 0.0)
            mixed = inner + jnp.where(match, carried, 0.0)
            scale = lax.rsqrt(jnp.mean(mixed * mixed, axis=-1, keepdims=True) + 1e-06)
            mixed_rows[d, :, cols] = (mixed * scale * gains[h]).astype(jnp.bfloat16)
        return last_doc

    copies = []
    for d in range(count):
        carry_doc = block(d, carry_doc)
        if d + 1 in (count // 2, count):
            done = pl.ds(0, count // 2) if d + 1 < count else pl.ds(count // 2, count - count // 2)
            copies += start_all(
                [
                    pltpu.make_async_copy(
                        mixed_rows.at[done, rows_of(peer, share), :],
                        outs[m].at[done],
                        sems.at[int(d + 1 == count), m],
                    )
                    for m, peer in enumerate(peers(pairs))
                ]
            )
    if not last:
        kept[0][...] = carry_doc
        kept[1][...] = state[...]
    wait_all(copies)


def attend(pairs, share, width, first, count, last, gain, queries, own, other, given):
    half, dtype = pairs * share, own.dtype
    state = (width // HEAD_DIM, HEAD_DIM, HEAD_DIM)
    kept = [
        jax.ShapeDtypeStruct((1, SPAN), jnp.float32),
        jax.ShapeDtypeStruct(state, jnp.float32),
        jax.ShapeDtypeStruct((2 * half, SPAN), dtype),
    ]
    kept, given = [] if last else kept, list(given) if first else []
    near = [
        pltpu.with_memory_space_constraint(x, pltpu.VMEM)
        for x in given + [queries, own, other]
    ]
    results = pl.pallas_call(
        functools.partial(attend_kernel, pairs, share, width, first, count, last),
        out_shape=[jax.ShapeDtypeStruct((count, share, width), dtype)] * pairs + kept,
        in_specs=[VMEM] * (4 + len(given)),
        out_specs=[ANY] * pairs + [VMEM] * len(kept),
        scratch_shapes=[
            pltpu.VMEM(state, jnp.float32),
            pltpu.VMEM((count, half, width), dtype),
            pltpu.SemaphoreType.DMA((2, pairs)),
        ],
        compiler_params=ROOM,
        name="attend",
    )(gain, *near)
    return results[:pairs], results[pairs:]


def unpack_kernel(pairs, width, spans, *rest):
    out_ref, sems = rest[-2:]
    copies = []
    for c, (first, count) in enumerate(spans):
        for m, peer in enumerate(peers(pairs)):
            come = pl.ds(pl.multiple_of(peer * width, width), width)
            copies.append(
                pltpu.make_async_copy(
                    rest[c * pairs + m], out_ref.at[pl.ds(first, count), :, come], sems.at[c, m]
                )
            )
    wait_all(start_all(copies))


def unpack(n, width, spans, pieces):
    share, dtype = pieces[0].shape[1], pieces[0].dtype
    pairs = n // 2
    return pl.pallas_call(
        functools.partial(unpack_kernel, pairs, width, spans),
        out_shape=jax.ShapeDtypeStruct((n, share, pairs * width), dtype),
        in_specs=[ANY] * (pairs * len(spans)),
        out_specs=ANY,
        scratch_shapes=[pltpu.SemaphoreType.DMA((len(spans), pairs))],
        compiler_params=ROOM,
        name="unpack",
    )(*pieces)


def swap(x, n, zero, one):
    return lax.ppermute(x, AXIS, [(i, i ^ (one if i & 1 else zero)) for i in range(n)])


def exchange(n, pieces):
    arrived = []
    for (zero, one), x in zip(slots(n // 2), pieces):
        arrived.append(swap(x, n, 2 * zero, 2 * one) if zero else x)
    return arrived


def heads_apart(n, q_store, k_store, v_store, plan, doc_ids, gain):
    share, pairs, full = SPAN // n, n // 2, q_store.shape[1]
    width = full // pairs
    stays = lambda a, *shape: pltpu.with_memory_space_constraint(a.reshape(shape), pltpu.HBM)
    heads = full // HEAD_DIM
    tiled = lambda a: a.reshape(n, share, heads, HEAD_DIM).transpose(0, 2, 1, 3)
    q, k, v = (stays(tiled(a), n, heads, share, HEAD_DIM) for a in (q_store, k_store, v_store))
    plan, docs = stays(plan, 1, SPAN), stays(doc_ids, 1, SPAN)
    gain = gain.reshape(heads, HEAD_DIM)
    parts = [c * n // sum(CHUNKS) for c in CHUNKS]
    spans = [(sum(parts[:c]), count) for c, count in enumerate(parts)]
    arrived = []
    for first, count in spans:
        pieces = pack(pairs, first, count, plan, docs, q, k, v)
        arrived.append(exchange(n, pieces))
    back, given, marked = [], None, []
    for (first, count), pieces in zip(spans, arrived):
        last = first + count == n
        marks = marked
        if not last:
            marks = marks + [mark(plan)]
        tiles = count * heads // pairs
        own = collect(pairs, tiles, pieces[0].shape[0], pieces, marks)
        other = swap(own, n, 1, 1)
        queries = collect(pairs, 0, tiles, pieces, [])
        pieces, given = attend(
            pairs, share, width, first, count, last, gain, queries, own, other, given
        )
        if not last:
            marked = [mark(pieces[-1])]
        back += exchange(n, pieces)
    return unpack(n, width, spans, back).reshape(SPAN, full)


def solution(mesh):
    n = mesh.shape[AXIS]

    def on_device(q_store, k_store, v_store, plan, doc_ids, gain):
        heads = q_store.shape[1] // HEAD_DIM
        paired = n & (n - 1) == 0
        tiled = q_store.shape[0] == SPAN and SPAN % n == 0 and (SPAN // n) % 8 == 0
        if paired and tiled and n >= 8 and heads % n == 0:
            return heads_apart(n, q_store, k_store, v_store, plan, doc_ids, gain)
        return at_home(q_store, k_store, v_store, plan, doc_ids, gain)

    return jax.shard_map(
        on_device,
        mesh=mesh,
        in_specs=(
            P(("groups", "context"), None),
            P(("groups", "context"), None),
            P(("groups", "context"), None),
            P(("groups", "context"), None),
            P(("groups", "context")),
            P(),
        ),
        out_specs=P(("groups", "context"), None),
        check_vma=False,
    )
```

profile of v0, /device:TPU:1, one launch (start us, length us, event | category | flops | bytes accessed | tf_op | source)
XLA Modules:
  0.0 114.7 jit_solution(9134042049138870167)
XLA Ops:
  0.0 2.0 %pack.2 = (bf16[121,8,128]{2,1,0:T(8,128)(2,1)S(1)}, bf16[121,8,128]{2,1,0:T(8,128)(2,1)S(1)}, bf16[121,8,128]{2,1,0:T(8,128)(2,1)S(1)}, bf16[121,8,128]{2,1,0:T...) custom-call(s32[1,128]{1,0:T(1,128)} %plan_ref.3, ...), custom_call_target="tpu_custom_call" | custom-call | tf_op jit(solution)/shard_map/pack/pallas_call | solution.py:190
  2.0 2.1 %collective-permute-start = (bf16[121,8,128]{2,1,0:T(8,128)(2,1)S(1)}, bf16[121,8,128]{2,1,0:T(8,128)(2,1)S(1)}, u32[]{:S(2)}, u32[]{:S(2)}) collective-permute-start(bf16[121,8,128]{2,1,0:T(8,128)(2,1)S(1)} %get-tuple-element.40), channel_id=1, source_target_pairs={{0,14},{1,3},{2,12},{3,1},{4,10},{5,7},{6,8},{7,5},{8,6},{9,11},{1... | collective-permute-start | bytes 743432 | tf_op jit(solution)/shard_map/ppermute | solution.py:391
  4.1 1.2 %collective-permute-start.1 = (bf16[121,8,128]{2,1,0:T(8,128)(2,1)S(1)}, bf16[121,8,128]{2,1,0:T(8,128)(2,1)S(1)}, u32[]{:S(2)}, u32[]{:S(2)}) collective-permute-start(bf16[121,8,128]{2,1,0:T(8,128)(2,1)S(1)} %get-tuple-element.41), channel_id=1, source_target_pairs={{0,12},{1,7},{2,14},{3,5},{4,8},{5,3},{6,10},{7,1},{8,4},{9,15},{1... | collective-permute-start | bytes 743432 | tf_op jit(solution)/shard_map/ppermute | solution.py:391
  5.4 0.1 collective-permute-start.2
  5.4 4.4 %collective-permute-start.3 = (bf16[121,8,128]{2,1,0:T(8,128)(2,1)S(1)}, bf16[121,8,128]{2,1,0:T(8,128)(2,1)S(1)}, u32[]{:S(2)}, u32[]{:S(2)}) collective-permute-start(bf16[121,8,128]{2,1,0:T(8,128)(2,1)S(1)} %get-tuple-element.43), channel_id=1, source_target_pairs={{0,8},{1,15},{2,10},{3,13},{4,12},{5,11},{6,14},{7,9},{8,0},{9,7},... | collective-permute-start | bytes 743432 | tf_op jit(solution)/shard_map/ppermute | solution.py:391
  9.8 2.8 %collective-permute-done.rest_0_.rest_1_ = bf16[121,8,128]{2,1,0:T(8,128)(2,1)S(1)} collective-permute-done((bf16[121,8,128]{2,1,0:T(8,128)(2,1)S(1)}, bf16[121,8,128]{2,1,0:T(8,128)(2,1)S(1)}, u32[]{:S(2)}, u32[]{:S(2)}) %collective-permute-start) | collective-permute-done | bytes 247840 | tf_op jit(solution)/shard_map/ppermute | solution.py:391
  12.6 7.3 %collective-permute-start.5 = (bf16[121,8,128]{2,1,0:T(8,128)(2,1)S(1)}, bf16[121,8,128]{2,1,0:T(8,128)(2,1)S(1)}, u32[]{:S(2)}, u32[]{:S(2)}) collective-permute-start(bf16[121,8,128]{2,1,0:T(8,128)(2,1)S(1)} %get-tuple-element.45), channel_id=1, source_target_pairs={{0,6},{1,11},{2,4},{3,9},{4,2},{5,15},{6,0},{7,13},{8,14},{9,3},{1... | collective-permute-start | bytes 743432 | tf_op jit(solution)/shard_map/ppermute | solution.py:391
  19.9 5.5 %collective-permute-done.3.rest_3_.rest_4_ = bf16[121,8,128]{2,1,0:T(8,128)(2,1)S(1)} collective-permute-done((bf16[121,8,128]{2,1,0:T(8,128)(2,1)S(1)}, bf16[121,8,128]{2,1,0:T(8,128)(2,1)S(1)}, u32[]{:S(2)}, u32[]{:S(2)}) %collective-permute-start.3) | collective-permute-done | bytes 247840 | tf_op jit(solution)/shard_map/ppermute | solution.py:391
  25.4 3.8 %collective-permute-done.4.rest_4_.rest_5_ = bf16[121,8,128]{2,1,0:T(8,128)(2,1)S(1)} collective-permute-done((bf16[121,8,128]{2,1,0:T(8,128)(2,1)S(1)}, bf16[121,8,128]{2,1,0:T(8,128)(2,1)S(1)}, u32[]{:S(2)}, u32[]{:S(2)}) %collective-permute-start.4) | collective-permute-done | bytes 247840 | tf_op jit(solution)/shard_map/ppermute | solution.py:391
  29.2 17.3 %collective-permute-done.5.rest_5_.rest_6_ = bf16[121,8,128]{2,1,0:T(8,128)(2,1)S(1)} collective-permute-done((bf16[121,8,128]{2,1,0:T(8,128)(2,1)S(1)}, bf16[121,8,128]{2,1,0:T(8,128)(2,1)S(1)}, u32[]{:S(2)}, u32[]{:S(2)}) %collective-permute-start.5) | collective-permute-done | bytes 247840 | tf_op jit(solution)/shard_map/ppermute | solution.py:391
  46.5 4.5 %collective-permute-done.6.rest_6_.rest_7_ = bf16[121,8,128]{2,1,0:T(8,128)(2,1)S(1)} collective-permute-done((bf16[121,8,128]{2,1,0:T(8,128)(2,1)S(1)}, bf16[121,8,128]{2,1,0:T(8,128)(2,1)S(1)}, u32[]{:S(2)}, u32[]{:S(2)}) %collective-permute-start.6) | collective-permute-done | bytes 247840 | tf_op jit(solution)/shard_map/ppermute | solution.py:391
  51.0 0.5 collect.5.rest_1_
  51.5 3.2 %collective-permute-start.7 = (bf16[81,64,128]{2,1,0:T(8,128)(2,1)S(1)}, bf16[81,64,128]{2,1,0:T(8,128)(2,1)S(1)}, u32[]{:S(2)}, u32[]{:S(2)}) collective-permute-start(bf16[81,64,128]{2,1,0:T(8,128)(2,1)S(1)} %collect.5.rest_1_), channel_id=1, source_target_pairs={{0,1},{1,0},{2,3},{3,2},{4,5},{5,4},{6,7},{7,6},{8,9},{9,8},{10,11... | collective-permute-start | bytes 3981320 | tf_op jit(solution)/shard_map/ppermute | solution.py:391
  54.7 1.6 %pack.3 = (bf16[72,8,128]{2,1,0:T(8,128)(2,1)S(1)}, bf16[72,8,128]{2,1,0:T(8,128)(2,1)S(1)}, bf16[72,8,128]{2,1,0:T(8,128)(2,1)S(1)}, bf16[72,8,128]{2,1,0:T(8,1...) custom-call(s32[1,128]{1,0:T(1,128)} %plan_ref.3, ...), custom_call_target="tpu_custom_call" | custom-call | tf_op jit(solution)/shard_map/pack/pallas_call | solution.py:190
  56.3 0.4 collective-permute-start.15
  56.7 0.1 collective-permute-start.16
  56.8 2.2 %collective-permute-start.17 = (bf16[72,8,128]{2,1,0:T(8,128)(2,1)S(1)}, bf16[72,8,128]{2,1,0:T(8,128)(2,1)S(1)}, u32[]{:S(2)}, u32[]{:S(2)}) collective-permute-start(bf16[72,8,128]{2,1,0:T(8,128)(2,1)S(1)} %get-tuple-element.61), channel_id=1, source_target_pairs={{0,10},{1,5},{2,8},{3,7},{4,14},{5,1},{6,12},{7,3},{8,2},{9,13},{1... | collective-permute-start | bytes 442376 | tf_op jit(solution)/shard_map/ppermute | solution.py:391
  59.0 2.3 %collective-permute-start.18 = (bf16[72,8,128]{2,1,0:T(8,128)(2,1)S(1)}, bf16[72,8,128]{2,1,0:T(8,128)(2,1)S(1)}, u32[]{:S(2)}, u32[]{:S(2)}) collective-permute-start(bf16[72,8,128]{2,1,0:T(8,128)(2,1)S(1)} %get-tuple-element.62), channel_id=1, source_target_pairs={{0,8},{1,15},{2,10},{3,13},{4,12},{5,11},{6,14},{7,9},{8,0},{9,7},... | collective-permute-start | bytes 442376 | tf_op jit(solution)/shard_map/ppermute | solution.py:391
  61.3 0.7 collective-permute-done.15.rest_0_.rest_1_
  61.9 2.3 %collective-permute-start.19 = (bf16[72,8,128]{2,1,0:T(8,128)(2,1)S(1)}, bf16[72,8,128]{2,1,0:T(8,128)(2,1)S(1)}, u32[]{:S(2)}, u32[]{:S(2)}) collective-permute-start(bf16[72,8,128]{2,1,0:T(8,128)(2,1)S(1)} %get-tuple-element.63), channel_id=1, source_target_pairs={{0,2},{1,13},{2,0},{3,15},{4,6},{5,9},{6,4},{7,11},{8,10},{9,5},{1... | collective-permute-start | bytes 442376 | tf_op jit(solution)/shard_map/ppermute | solution.py:391
  64.2 0.2 collective-permute-start.20
  64.4 1.4 %collective-permute-start.21 = (bf16[72,8,128]{2,1,0:T(8,128)(2,1)S(1)}, bf16[72,8,128]{2,1,0:T(8,128)(2,1)S(1)}, u32[]{:S(2)}, u32[]{:S(2)}) collective-permute-start(bf16[72,8,128]{2,1,0:T(8,128)(2,1)S(1)} %get-tuple-element.65), channel_id=1, source_target_pairs={{0,4},{1,9},{2,6},{3,11},{4,0},{5,13},{6,2},{7,15},{8,12},{9,1},{1... | collective-permute-start | bytes 442376 | tf_op jit(solution)/shard_map/ppermute | solution.py:391
  65.8 0.3 collect.4.rest_0_
  66.1 2.7 %attend.2 = (bf16[10,8,512]{2,1,0:T(8,128)(2,1)S(1)}, bf16[10,8,512]{2,1,0:T(8,128)(2,1)S(1)}, bf16[10,8,512]{2,1,0:T(8,128)(2,1)S(1)}, bf16[10,8,512]{2,1,0:T(8...) custom-call(f32[32,128]{1,0:T(8,128)S(1)} %bitcast.12, ...), custom_call_target="tpu_custom_call" | custom-call | tf_op jit(solution)/shard_map/attend/pallas_call | solution.py:346
  68.9 0.6 collective-permute-done.18.rest_3_.rest_4_
  69.4 2.7 %collective-permute-done.19.rest_4_.rest_5_ = bf16[72,8,128]{2,1,0:T(8,128)(2,1)S(1)} collective-permute-done((bf16[72,8,128]{2,1,0:T(8,128)(2,1)S(1)}, bf16[72,8,128]{2,1,0:T(8,128)(2,1)S(1)}, u32[]{:S(2)}, u32[]{:S(2)}) %collective-permute-start.19) | collective-permute-done | bytes 147488 | tf_op jit(solution)/shard_map/ppermute | solution.py:391
  72.1 10.9 %collective-permute-done.20.rest_5_.rest_6_ = bf16[72,8,128]{2,1,0:T(8,128)(2,1)S(1)} collective-permute-done((bf16[72,8,128]{2,1,0:T(8,128)(2,1)S(1)}, bf16[72,8,128]{2,1,0:T(8,128)(2,1)S(1)}, u32[]{:S(2)}, u32[]{:S(2)}) %collective-permute-start.20) | collective-permute-done | bytes 147488 | tf_op jit(solution)/shard_map/ppermute | solution.py:391
  83.0 0.6 collective-permute-done.21.rest_6_.rest_7_
  83.6 0.3 collect.7.rest_4_
  83.9 0.1 collective-permute-start.22
  84.0 1.3 %collective-permute-start.8 = (bf16[10,8,512]{2,1,0:T(8,128)(2,1)S(1)}, bf16[10,8,512]{2,1,0:T(8,128)(2,1)S(1)}, u32[]{:S(2)}, u32[]{:S(2)}) collective-permute-start(bf16[10,8,512]{2,1,0:T(8,128)(2,1)S(1)} %get-tuple-element.48), channel_id=1, source_target_pairs={{0,14},{1,3},{2,12},{3,1},{4,10},{5,7},{6,8},{7,5},{8,6},{9,11},{1... | collective-permute-start | bytes 245768 | tf_op jit(solution)/shard_map/ppermute | solution.py:391
  85.3 1.4 %collective-permute-start.10 = (bf16[10,8,512]{2,1,0:T(8,128)(2,1)S(1)}, bf16[10,8,512]{2,1,0:T(8,128)(2,1)S(1)}, u32[]{:S(2)}, u32[]{:S(2)}) collective-permute-start(bf16[10,8,512]{2,1,0:T(8,128)(2,1)S(1)} %get-tuple-element.50), channel_id=1, source_target_pairs={{0,10},{1,5},{2,8},{3,7},{4,14},{5,1},{6,12},{7,3},{8,2},{9,13},{1... | collective-permute-start | bytes 245768 | tf_op jit(solution)/shard_map/ppermute | solution.py:391
  86.7 3.2 %collective-permute-start.11 = (bf16[10,8,512]{2,1,0:T(8,128)(2,1)S(1)}, bf16[10,8,512]{2,1,0:T(8,128)(2,1)S(1)}, u32[]{:S(2)}, u32[]{:S(2)}) collective-permute-start(bf16[10,8,512]{2,1,0:T(8,128)(2,1)S(1)} %get-tuple-element.51), channel_id=1, source_target_pairs={{0,8},{1,15},{2,10},{3,13},{4,12},{5,11},{6,14},{7,9},{8,0},{9,7},... | collective-permute-start | bytes 245768 | tf_op jit(solution)/shard_map/ppermute | solution.py:391
  90.0 1.0 collective-permute-start.12
  91.0 2.3 %collective-permute-start.14 = (bf16[10,8,512]{2,1,0:T(8,128)(2,1)S(1)}, bf16[10,8,512]{2,1,0:T(8,128)(2,1)S(1)}, u32[]{:S(2)}, u32[]{:S(2)}) collective-permute-start(bf16[10,8,512]{2,1,0:T(8,128)(2,1)S(1)} %get-tuple-element.54), channel_id=1, source_target_pairs={{0,4},{1,9},{2,6},{3,11},{4,0},{5,13},{6,2},{7,15},{8,12},{9,1},{1... | collective-permute-start | bytes 245768 | tf_op jit(solution)/shard_map/ppermute | solution.py:391
  93.3 0.2 collect.6.rest_3_
  93.5 2.1 %attend.3 = (bf16[6,8,512]{2,1,0:T(8,128)(2,1)S(1)}, bf16[6,8,512]{2,1,0:T(8,128)(2,1)S(1)}, bf16[6,8,512]{2,1,0:T(8,128)(2,1)S(1)}, bf16[6,8,512]{2,1,0:T(8,128...) custom-call(f32[32,128]{1,0:T(8,128)S(1)} %bitcast.13, ...), custom_call_target="tpu_custom_call" | custom-call | tf_op jit(solution)/shard_map/attend/pallas_call | solution.py:346
  95.6 1.3 %collective-permute-start.23 = (bf16[6,8,512]{2,1,0:T(8,128)(2,1)S(1)}, bf16[6,8,512]{2,1,0:T(8,128)(2,1)S(1)}, u32[]{:S(2)}, u32[]{:S(2)}) collective-permute-start(bf16[6,8,512]{2,1,0:T(8,128)(2,1)S(1)} %get-tuple-element.67), channel_id=1, source_target_pairs={{0,14},{1,3},{2,12},{3,1},{4,10},{5,7},{6,8},{7,5},{8,6},{9,11},{1... | collective-permute-start | bytes 147464 | tf_op jit(solution)/shard_map/ppermute | solution.py:391
  96.9 0.2 collective-permute-start.24
  97.1 2.6 %collective-permute-start.25 = (bf16[6,8,512]{2,1,0:T(8,128)(2,1)S(1)}, bf16[6,8,512]{2,1,0:T(8,128)(2,1)S(1)}, u32[]{:S(2)}, u32[]{:S(2)}) collective-permute-start(bf16[6,8,512]{2,1,0:T(8,128)(2,1)S(1)} %get-tuple-element.69), channel_id=1, source_target_pairs={{0,10},{1,5},{2,8},{3,7},{4,14},{5,1},{6,12},{7,3},{8,2},{9,13},{1... | collective-permute-start | bytes 147464 | tf_op jit(solution)/shard_map/ppermute | solution.py:391
  99.7 1.2 %collective-permute-done.13.rest_5_ = bf16[10,8,512]{2,1,0:T(8,128)(2,1)S(1)} collective-permute-done((bf16[10,8,512]{2,1,0:T(8,128)(2,1)S(1)}, bf16[10,8,512]{2,1,0:T(8,128)(2,1)S(1)}, u32[]{:S(2)}, u32[]{:S(2)}) %collective-permute-start.13) | collective-permute-done | bytes 81952 | tf_op jit(solution)/shard_map/ppermute | solution.py:391
  101.0 3.5 %collective-permute-start.26 = (bf16[6,8,512]{2,1,0:T(8,128)(2,1)S(1)}, bf16[6,8,512]{2,1,0:T(8,128)(2,1)S(1)}, u32[]{:S(2)}, u32[]{:S(2)}) collective-permute-start(bf16[6,8,512]{2,1,0:T(8,128)(2,1)S(1)} %get-tuple-element.70), channel_id=1, source_target_pairs={{0,8},{1,15},{2,10},{3,13},{4,12},{5,11},{6,14},{7,9},{8,0},{9,7},... | collective-permute-start | bytes 147464 | tf_op jit(solution)/shard_map/ppermute | solution.py:391
  104.5 0.7 collective-permute-start.27
  105.2 2.3 %collective-permute-start.29 = (bf16[6,8,512]{2,1,0:T(8,128)(2,1)S(1)}, bf16[6,8,512]{2,1,0:T(8,128)(2,1)S(1)}, u32[]{:S(2)}, u32[]{:S(2)}) collective-permute-start(bf16[6,8,512]{2,1,0:T(8,128)(2,1)S(1)} %get-tuple-element.73), channel_id=1, source_target_pairs={{0,4},{1,9},{2,6},{3,11},{4,0},{5,13},{6,2},{7,15},{8,12},{9,1},{1... | collective-permute-start | bytes 147464 | tf_op jit(solution)/shard_map/ppermute | solution.py:391
  107.5 2.3 %collective-permute-done.27.rest_12_ = bf16[6,8,512]{2,1,0:T(8,128)(2,1)S(1)} collective-permute-done((bf16[6,8,512]{2,1,0:T(8,128)(2,1)S(1)}, bf16[6,8,512]{2,1,0:T(8,128)(2,1)S(1)}, u32[]{:S(2)}, u32[]{:S(2)}) %collective-permute-start.27) | collective-permute-done | bytes 49184 | tf_op jit(solution)/shard_map/ppermute | solution.py:391
  109.8 1.8 %collective-permute-done.28.rest_13_ = bf16[6,8,512]{2,1,0:T(8,128)(2,1)S(1)} collective-permute-done((bf16[6,8,512]{2,1,0:T(8,128)(2,1)S(1)}, bf16[6,8,512]{2,1,0:T(8,128)(2,1)S(1)}, u32[]{:S(2)}, u32[]{:S(2)}) %collective-permute-start.28) | collective-permute-done | bytes 49184 | tf_op jit(solution)/shard_map/ppermute | solution.py:391
  111.6 2.0 %collective-permute-done.29.rest_14_ = bf16[6,8,512]{2,1,0:T(8,128)(2,1)S(1)} collective-permute-done((bf16[6,8,512]{2,1,0:T(8,128)(2,1)S(1)}, bf16[6,8,512]{2,1,0:T(8,128)(2,1)S(1)}, u32[]{:S(2)}, u32[]{:S(2)}) %collective-permute-start.29) | collective-permute-done | bytes 49184 | tf_op jit(solution)/shard_map/ppermute | solution.py:391
  113.6 1.1 unpack.1
  (25 shorter events, 0.1 us)
Async XLA Ops:
  2.0 10.6 %collective-permute-start = (bf16[121,8,128]{2,1,0:T(8,128)(2,1)S(1)}, bf16[121,8,128]{2,1,0:T(8,128)(2,1)S(1)}, u32[]{:S(2)}, u32[]{:S(2)}) collective-permute-start(bf16[121,8,128]{2,1,0:T(8,128)(2,1)S(1)} %get-tuple-element.40), channel_id=1, source_target_pairs={{0,14},{1,3},{2,12},{3,1},{4,10},{5,7},{6,8},{7,5},{8,6},{9,11},{1... | collective-permute-start | bytes 743432 | tf_op jit(solution)/shard_map/ppermute | solution.py:391
  4.1 15.8 %collective-permute-start.1 = (bf16[121,8,128]{2,1,0:T(8,128)(2,1)S(1)}, bf16[121,8,128]{2,1,0:T(8,128)(2,1)S(1)}, u32[]{:S(2)}, u32[]{:S(2)}) collective-permute-start(bf16[121,8,128]{2,1,0:T(8,128)(2,1)S(1)} %get-tuple-element.41), channel_id=1, source_target_pairs={{0,12},{1,7},{2,14},{3,5},{4,8},{5,3},{6,10},{7,1},{8,4},{9,15},{1... | collective-permute-start | bytes 743432 | tf_op jit(solution)/shard_map/ppermute | solution.py:391
  5.4 14.5 %collective-permute-start.2 = (bf16[121,8,128]{2,1,0:T(8,128)(2,1)S(1)}, bf16[121,8,128]{2,1,0:T(8,128)(2,1)S(1)}, u32[]{:S(2)}, u32[]{:S(2)}) collective-permute-start(bf16[121,8,128]{2,1,0:T(8,128)(2,1)S(1)} %get-tuple-element.42), channel_id=1, source_target_pairs={{0,10},{1,5},{2,8},{3,7},{4,14},{5,1},{6,12},{7,3},{8,2},{9,13},{1... | collective-permute-start | bytes 743432 | tf_op jit(solution)/shard_map/ppermute | solution.py:391
  5.4 20.0 %collective-permute-start.3 = (bf16[121,8,128]{2,1,0:T(8,128)(2,1)S(1)}, bf16[121,8,128]{2,1,0:T(8,128)(2,1)S(1)}, u32[]{:S(2)}, u32[]{:S(2)}) collective-permute-start(bf16[121,8,128]{2,1,0:T(8,128)(2,1)S(1)} %get-tuple-element.43), channel_id=1, source_target_pairs={{0,8},{1,15},{2,10},{3,13},{4,12},{5,11},{6,14},{7,9},{8,0},{9,7},... | collective-permute-start | bytes 743432 | tf_op jit(solution)/shard_map/ppermute | solution.py:391
  9.8 19.3 %collective-permute-start.4 = (bf16[121,8,128]{2,1,0:T(8,128)(2,1)S(1)}, bf16[121,8,128]{2,1,0:T(8,128)(2,1)S(1)}, u32[]{:S(2)}, u32[]{:S(2)}) collective-permute-start(bf16[121,8,128]{2,1,0:T(8,128)(2,1)S(1)} %get-tuple-element.44), channel_id=1, source_target_pairs={{0,2},{1,13},{2,0},{3,15},{4,6},{5,9},{6,4},{7,11},{8,10},{9,5},{1... | collective-permute-start | bytes 743432 | tf_op jit(solution)/shard_map/ppermute | solution.py:391
  12.6 33.9 %collective-permute-start.5 = (bf16[121,8,128]{2,1,0:T(8,128)(2,1)S(1)}, bf16[121,8,128]{2,1,0:T(8,128)(2,1)S(1)}, u32[]{:S(2)}, u32[]{:S(2)}) collective-permute-start(bf16[121,8,128]{2,1,0:T(8,128)(2,1)S(1)} %get-tuple-element.45), channel_id=1, source_target_pairs={{0,6},{1,11},{2,4},{3,9},{4,2},{5,15},{6,0},{7,13},{8,14},{9,3},{1... | collective-permute-start | bytes 743432 | tf_op jit(solution)/shard_map/ppermute | solution.py:391
  19.9 31.1 %collective-permute-start.6 = (bf16[121,8,128]{2,1,0:T(8,128)(2,1)S(1)}, bf16[121,8,128]{2,1,0:T(8,128)(2,1)S(1)}, u32[]{:S(2)}, u32[]{:S(2)}) collective-permute-start(bf16[121,8,128]{2,1,0:T(8,128)(2,1)S(1)} %get-tuple-element.46), channel_id=1, source_target_pairs={{0,4},{1,9},{2,6},{3,11},{4,0},{5,13},{6,2},{7,15},{8,12},{9,1},{1... | collective-permute-start | bytes 743432 | tf_op jit(solution)/shard_map/ppermute | solution.py:391
  51.5 12.9 %collective-permute-start.7 = (bf16[81,64,128]{2,1,0:T(8,128)(2,1)S(1)}, bf16[81,64,128]{2,1,0:T(8,128)(2,1)S(1)}, u32[]{:S(2)}, u32[]{:S(2)}) collective-permute-start(bf16[81,64,128]{2,1,0:T(8,128)(2,1)S(1)} %collect.5.rest_1_), channel_id=1, source_target_pairs={{0,1},{1,0},{2,3},{3,2},{4,5},{5,4},{6,7},{7,6},{8,9},{9,8},{10,11... | collective-permute-start | bytes 3981320 | tf_op jit(solution)/shard_map/ppermute | solution.py:391
  56.3 9.9 %copy-start = (f32[4096]{0:T(1024)S(1)}, f32[4096]{0:T(1024)}, u32[]{:S(2)}) copy-start(f32[4096]{0:T(1024)} %param.11) | copy-start | bytes 49156
  56.3 5.6 %collective-permute-start.15 = (bf16[72,8,128]{2,1,0:T(8,128)(2,1)S(1)}, bf16[72,8,128]{2,1,0:T(8,128)(2,1)S(1)}, u32[]{:S(2)}, u32[]{:S(2)}) collective-permute-start(bf16[72,8,128]{2,1,0:T(8,128)(2,1)S(1)} %get-tuple-element.59), channel_id=1, source_target_pairs={{0,14},{1,3},{2,12},{3,1},{4,10},{5,7},{6,8},{7,5},{8,6},{9,11},{1... | collective-permute-start | bytes 442376 | tf_op jit(solution)/shard_map/ppermute | solution.py:391
  56.7 7.5 %collective-permute-start.16 = (bf16[72,8,128]{2,1,0:T(8,128)(2,1)S(1)}, bf16[72,8,128]{2,1,0:T(8,128)(2,1)S(1)}, u32[]{:S(2)}, u32[]{:S(2)}) collective-permute-start(bf16[72,8,128]{2,1,0:T(8,128)(2,1)S(1)} %get-tuple-element.60), channel_id=1, source_target_pairs={{0,12},{1,7},{2,14},{3,5},{4,8},{5,3},{6,10},{7,1},{8,4},{9,15},{1... | collective-permute-start | bytes 442376 | tf_op jit(solution)/shard_map/ppermute | solution.py:391
  56.8 12.1 %collective-permute-start.17 = (bf16[72,8,128]{2,1,0:T(8,128)(2,1)S(1)}, bf16[72,8,128]{2,1,0:T(8,128)(2,1)S(1)}, u32[]{:S(2)}, u32[]{:S(2)}) collective-permute-start(bf16[72,8,128]{2,1,0:T(8,128)(2,1)S(1)} %get-tuple-element.61), channel_id=1, source_target_pairs={{0,10},{1,5},{2,8},{3,7},{4,14},{5,1},{6,12},{7,3},{8,2},{9,13},{1... | collective-permute-start | bytes 442376 | tf_op jit(solution)/shard_map/ppermute | solution.py:391
  59.0 10.4 %collective-permute-start.18 = (bf16[72,8,128]{2,1,0:T(8,128)(2,1)S(1)}, bf16[72,8,128]{2,1,0:T(8,128)(2,1)S(1)}, u32[]{:S(2)}, u32[]{:S(2)}) collective-permute-start(bf16[72,8,128]{2,1,0:T(8,128)(2,1)S(1)} %get-tuple-element.62), channel_id=1, source_target_pairs={{0,8},{1,15},{2,10},{3,13},{4,12},{5,11},{6,14},{7,9},{8,0},{9,7},... | collective-permute-start | bytes 442376 | tf_op jit(solution)/shard_map/ppermute | solution.py:391
  61.9 10.2 %collective-permute-start.19 = (bf16[72,8,128]{2,1,0:T(8,128)(2,1)S(1)}, bf16[72,8,128]{2,1,0:T(8,128)(2,1)S(1)}, u32[]{:S(2)}, u32[]{:S(2)}) collective-permute-start(bf16[72,8,128]{2,1,0:T(8,128)(2,1)S(1)} %get-tuple-element.63), channel_id=1, source_target_pairs={{0,2},{1,13},{2,0},{3,15},{4,6},{5,9},{6,4},{7,11},{8,10},{9,5},{1... | collective-permute-start | bytes 442376 | tf_op jit(solution)/shard_map/ppermute | solution.py:391
  64.2 18.8 %collective-permute-start.20 = (bf16[72,8,128]{2,1,0:T(8,128)(2,1)S(1)}, bf16[72,8,128]{2,1,0:T(8,128)(2,1)S(1)}, u32[]{:S(2)}, u32[]{:S(2)}) collective-permute-start(bf16[72,8,128]{2,1,0:T(8,128)(2,1)S(1)} %get-tuple-element.64), channel_id=1, source_target_pairs={{0,6},{1,11},{2,4},{3,9},{4,2},{5,15},{6,0},{7,13},{8,14},{9,3},{1... | collective-permute-start | bytes 442376 | tf_op jit(solution)/shard_map/ppermute | solution.py:391
  64.4 19.2 %collective-permute-start.21 = (bf16[72,8,128]{2,1,0:T(8,128)(2,1)S(1)}, bf16[72,8,128]{2,1,0:T(8,128)(2,1)S(1)}, u32[]{:S(2)}, u32[]{:S(2)}) collective-permute-start(bf16[72,8,128]{2,1,0:T(8,128)(2,1)S(1)} %get-tuple-element.65), channel_id=1, source_target_pairs={{0,4},{1,9},{2,6},{3,11},{4,0},{5,13},{6,2},{7,15},{8,12},{9,1},{1... | collective-permute-start | bytes 442376 | tf_op jit(solution)/shard_map/ppermute | solution.py:391
  83.9 7.0 %collective-permute-start.22 = (bf16[48,64,128]{2,1,0:T(8,128)(2,1)S(1)}, bf16[48,64,128]{2,1,0:T(8,128)(2,1)S(1)}, u32[]{:S(2)}, u32[]{:S(2)}) collective-permute-start(bf16[48,64,128]{2,1,0:T(8,128)(2,1)S(1)} %collect.7.rest_4_), channel_id=1, source_target_pairs={{0,1},{1,0},{2,3},{3,2},{4,5},{5,4},{6,7},{7,6},{8,9},{9,8},{10,11... | collective-permute-start | bytes 2359304 | tf_op jit(solution)/shard_map/ppermute | solution.py:391
  84.0 5.9 %collective-permute-start.8 = (bf16[10,8,512]{2,1,0:T(8,128)(2,1)S(1)}, bf16[10,8,512]{2,1,0:T(8,128)(2,1)S(1)}, u32[]{:S(2)}, u32[]{:S(2)}) collective-permute-start(bf16[10,8,512]{2,1,0:T(8,128)(2,1)S(1)} %get-tuple-element.48), channel_id=1, source_target_pairs={{0,14},{1,3},{2,12},{3,1},{4,10},{5,7},{6,8},{7,5},{8,6},{9,11},{1... | collective-permute-start | bytes 245768 | tf_op jit(solution)/shard_map/ppermute | solution.py:391
  85.3 5.6 %collective-permute-start.9 = (bf16[10,8,512]{2,1,0:T(8,128)(2,1)S(1)}, bf16[10,8,512]{2,1,0:T(8,128)(2,1)S(1)}, u32[]{:S(2)}, u32[]{:S(2)}) collective-permute-start(bf16[10,8,512]{2,1,0:T(8,128)(2,1)S(1)} %get-tuple-element.49), channel_id=1, source_target_pairs={{0,12},{1,7},{2,14},{3,5},{4,8},{5,3},{6,10},{7,1},{8,4},{9,15},{1... | collective-permute-start | bytes 245768 | tf_op jit(solution)/shard_map/ppermute | solution.py:391
  85.3 10.3 %collective-permute-start.10 = (bf16[10,8,512]{2,1,0:T(8,128)(2,1)S(1)}, bf16[10,8,512]{2,1,0:T(8,128)(2,1)S(1)}, u32[]{:S(2)}, u32[]{:S(2)}) collective-permute-start(bf16[10,8,512]{2,1,0:T(8,128)(2,1)S(1)} %get-tuple-element.50), channel_id=1, source_target_pairs={{0,10},{1,5},{2,8},{3,7},{4,14},{5,1},{6,12},{7,3},{8,2},{9,13},{1... | collective-permute-start | bytes 245768 | tf_op jit(solution)/shard_map/ppermute | solution.py:391
  86.7 10.2 %collective-permute-start.11 = (bf16[10,8,512]{2,1,0:T(8,128)(2,1)S(1)}, bf16[10,8,512]{2,1,0:T(8,128)(2,1)S(1)}, u32[]{:S(2)}, u32[]{:S(2)}) collective-permute-start(bf16[10,8,512]{2,1,0:T(8,128)(2,1)S(1)} %get-tuple-element.51), channel_id=1, source_target_pairs={{0,8},{1,15},{2,10},{3,13},{4,12},{5,11},{6,14},{7,9},{8,0},{9,7},... | collective-permute-start | bytes 245768 | tf_op jit(solution)/shard_map/ppermute | solution.py:391
  90.0 7.2 %collective-permute-start.12 = (bf16[10,8,512]{2,1,0:T(8,128)(2,1)S(1)}, bf16[10,8,512]{2,1,0:T(8,128)(2,1)S(1)}, u32[]{:S(2)}, u32[]{:S(2)}) collective-permute-start(bf16[10,8,512]{2,1,0:T(8,128)(2,1)S(1)} %get-tuple-element.52), channel_id=1, source_target_pairs={{0,2},{1,13},{2,0},{3,15},{4,6},{5,9},{6,4},{7,11},{8,10},{9,5},{1... | collective-permute-start | bytes 245768 | tf_op jit(solution)/shard_map/ppermute | solution.py:391
  91.0 10.0 %collective-permute-start.13 = (bf16[10,8,512]{2,1,0:T(8,128)(2,1)S(1)}, bf16[10,8,512]{2,1,0:T(8,128)(2,1)S(1)}, u32[]{:S(2)}, u32[]{:S(2)}) collective-permute-start(bf16[10,8,512]{2,1,0:T(8,128)(2,1)S(1)} %get-tuple-element.53), channel_id=1, source_target_pairs={{0,6},{1,11},{2,4},{3,9},{4,2},{5,15},{6,0},{7,13},{8,14},{9,3},{1... | collective-permute-start | bytes 245768 | tf_op jit(solution)/shard_map/ppermute | solution.py:391
  91.0 13.5 %collective-permute-start.14 = (bf16[10,8,512]{2,1,0:T(8,128)(2,1)S(1)}, bf16[10,8,512]{2,1,0:T(8,128)(2,1)S(1)}, u32[]{:S(2)}, u32[]{:S(2)}) collective-permute-start(bf16[10,8,512]{2,1,0:T(8,128)(2,1)S(1)} %get-tuple-element.54), channel_id=1, source_target_pairs={{0,4},{1,9},{2,6},{3,11},{4,0},{5,13},{6,2},{7,15},{8,12},{9,1},{1... | collective-permute-start | bytes 245768 | tf_op jit(solution)/shard_map/ppermute | solution.py:391
  95.6 9.6 %collective-permute-start.23 = (bf16[6,8,512]{2,1,0:T(8,128)(2,1)S(1)}, bf16[6,8,512]{2,1,0:T(8,128)(2,1)S(1)}, u32[]{:S(2)}, u32[]{:S(2)}) collective-permute-start(bf16[6,8,512]{2,1,0:T(8,128)(2,1)S(1)} %get-tuple-element.67), channel_id=1, source_target_pairs={{0,14},{1,3},{2,12},{3,1},{4,10},{5,7},{6,8},{7,5},{8,6},{9,11},{1... | collective-permute-start | bytes 147464 | tf_op jit(solution)/shard_map/ppermute | solution.py:391
  96.9 8.3 %collective-permute-start.24 = (bf16[6,8,512]{2,1,0:T(8,128)(2,1)S(1)}, bf16[6,8,512]{2,1,0:T(8,128)(2,1)S(1)}, u32[]{:S(2)}, u32[]{:S(2)}) collective-permute-start(bf16[6,8,512]{2,1,0:T(8,128)(2,1)S(1)} %get-tuple-element.68), channel_id=1, source_target_pairs={{0,12},{1,7},{2,14},{3,5},{4,8},{5,3},{6,10},{7,1},{8,4},{9,15},{1... | collective-permute-start | bytes 147464 | tf_op jit(solution)/shard_map/ppermute | solution.py:391
  97.1 10.4 %collective-permute-start.25 = (bf16[6,8,512]{2,1,0:T(8,128)(2,1)S(1)}, bf16[6,8,512]{2,1,0:T(8,128)(2,1)S(1)}, u32[]{:S(2)}, u32[]{:S(2)}) collective-permute-start(bf16[6,8,512]{2,1,0:T(8,128)(2,1)S(1)} %get-tuple-element.69), channel_id=1, source_target_pairs={{0,10},{1,5},{2,8},{3,7},{4,14},{5,1},{6,12},{7,3},{8,2},{9,13},{1... | collective-permute-start | bytes 147464 | tf_op jit(solution)/shard_map/ppermute | solution.py:391
  101.0 6.5 %collective-permute-start.26 = (bf16[6,8,512]{2,1,0:T(8,128)(2,1)S(1)}, bf16[6,8,512]{2,1,0:T(8,128)(2,1)S(1)}, u32[]{:S(2)}, u32[]{:S(2)}) collective-permute-start(bf16[6,8,512]{2,1,0:T(8,128)(2,1)S(1)} %get-tuple-element.70), channel_id=1, source_target_pairs={{0,8},{1,15},{2,10},{3,13},{4,12},{5,11},{6,14},{7,9},{8,0},{9,7},... | collective-permute-start | bytes 147464 | tf_op jit(solution)/shard_map/ppermute | solution.py:391
  104.5 5.3 %collective-permute-start.27 = (bf16[6,8,512]{2,1,0:T(8,128)(2,1)S(1)}, bf16[6,8,512]{2,1,0:T(8,128)(2,1)S(1)}, u32[]{:S(2)}, u32[]{:S(2)}) collective-permute-start(bf16[6,8,512]{2,1,0:T(8,128)(2,1)S(1)} %get-tuple-element.71), channel_id=1, source_target_pairs={{0,2},{1,13},{2,0},{3,15},{4,6},{5,9},{6,4},{7,11},{8,10},{9,5},{1... | collective-permute-start | bytes 147464 | tf_op jit(solution)/shard_map/ppermute | solution.py:391
  105.2 6.4 %collective-permute-start.28 = (bf16[6,8,512]{2,1,0:T(8,128)(2,1)S(1)}, bf16[6,8,512]{2,1,0:T(8,128)(2,1)S(1)}, u32[]{:S(2)}, u32[]{:S(2)}) collective-permute-start(bf16[6,8,512]{2,1,0:T(8,128)(2,1)S(1)} %get-tuple-element.72), channel_id=1, source_target_pairs={{0,6},{1,11},{2,4},{3,9},{4,2},{5,15},{6,0},{7,13},{8,14},{9,3},{1... | collective-permute-start | bytes 147464 | tf_op jit(solution)/shard_map/ppermute | solution.py:391
  105.2 8.4 %collective-permute-start.29 = (bf16[6,8,512]{2,1,0:T(8,128)(2,1)S(1)}, bf16[6,8,512]{2,1,0:T(8,128)(2,1)S(1)}, u32[]{:S(2)}, u32[]{:S(2)}) collective-permute-start(bf16[6,8,512]{2,1,0:T(8,128)(2,1)S(1)} %get-tuple-element.73), channel_id=1, source_target_pairs={{0,4},{1,9},{2,6},{3,11},{4,0},{5,13},{6,2},{7,15},{8,12},{9,1},{1... | collective-permute-start | bytes 147464 | tf_op jit(solution)/shard_map/ppermute | solution.py:391
where the time goes:
time: 116 us; the launch traced here: 115 us
  waiting for transfers between devices  56.6 us (49%)
  starting transfers between devices  47.2 us (41%)
  Pallas kernels  10.7 us (9%)
    ppermute x30, waiting for transfers between devices, swap(): lax.ppermute(x, AXIS, [(i, i ^ (one if i & 1 else zero)) for i in range(n)])  56.6 us
    ppermute x30, starting transfers between devices, swap(): lax.ppermute(x, AXIS, [(i, i ^ (one if i & 1 else zero)) for i in range(n)])  47.2 us
    pallas_call x2, Pallas kernels, attend(): pl.pallas_call(functools.partial(attend_kernel, pairs, share, width, firs...  4.77 us
    pallas_call x2, Pallas kernels, pack(): pl.pallas_call(functools.partial(pack_kernel, pairs, heads, first, count)...  3.56 us
  transfers between devices with their start and end apart: 30, of which 14 were waited for; matrix products, arithmetic and copies ran while one was open for 0% of the time, Pallas kernels for 6%

commit v1 on v0

--- a/solution.py
+++ b/solution.py
@@ -132,9 +132,9 @@
     return pl.ds(pl.multiple_of(pair * share, share), share)
 
 
-def pack_kernel(pairs, heads, first, count, plan_ref, doc_ref, q_ref, k_ref, v_ref, *rest):
-    pieces = rest[:pairs]
-    plans, docs, notes, sems, note_sems = rest[pairs:]
+def pack_kernel(pairs, heads, first, count, chosen, plan_ref, doc_ref, q_ref, k_ref, v_ref, *rest):
+    pieces = dict(zip(chosen, rest))
+    plans, docs, notes, sems, note_sems = rest[len(chosen) :]
     share = SPAN // (2 * pairs)
     copies = []
     if first == 0:
@@ -145,7 +145,7 @@
             ]
         )
     tiles = count * heads
-    for m, peer in enumerate(peers(pairs)):
+    for m, peer in ((m, peers(pairs)[m]) for m in chosen):
         for a, ref in enumerate((q_ref, k_ref, v_ref)):
             room = pieces[m].at[pl.ds(a * tiles, tiles)]
             copy = pltpu.make_async_copy(
@@ -177,21 +177,21 @@
         copies += start_all(
             [
                 pltpu.make_async_copy(notes, pieces[m].at[pl.ds(3 * tiles, 1)], note_sems.at[m])
-                for m in range(pairs)
+                for m in chosen
             ]
         )
     wait_all(copies)
 
 
-def pack(pairs, first, count, plan, docs, q, k, v):
+def pack(pairs, first, count, chosen, plan, docs, q, k, v):
     heads, share = q.shape[1] // pairs, q.shape[2]
     tiles = 3 * count * heads + (first == 0)
     shape = jax.ShapeDtypeStruct((tiles, share, HEAD_DIM), q.dtype)
     return pl.pallas_call(
-        functools.partial(pack_kernel, pairs, heads, first, count),
-        out_shape=[shape] * pairs,
+        functools.partial(pack_kernel, pairs, heads, first, count, chosen),
+        out_shape=[shape] * len(chosen),
         in_specs=[HBM] * 5,
-        out_specs=[ANY] * pairs,
+        out_specs=[ANY] * len(chosen),
         scratch_shapes=[
             pltpu.VMEM((1, SPAN), jnp.int32),
             pltpu.VMEM((1, SPAN), jnp.int32),
@@ -359,7 +359,8 @@
     return results[:pairs], results[pairs:]
 
 
-def unpack_kernel(pairs, width, spans, *rest):
+def unpack_kernel(pairs, width, spans, before, *rest):
+    pieces = rest[before:]
     out_ref, sems = rest[-2:]
     copies = []
     for c, (first, count) in enumerate(spans):
@@ -367,24 +368,27 @@
             come = pl.ds(pl.multiple_of(peer * width, width), width)
             copies.append(
                 pltpu.make_async_copy(
-                    rest[c * pairs + m], out_ref.at[pl.ds(first, count), :, come], sems.at[c, m]
+                    pieces[c * pairs + m],
+                    out_ref.at[pl.ds(first, count), :, come],
+                    sems.at[c, m],
                 )
             )
     wait_all(start_all(copies))
 
 
-def unpack(n, width, spans, pieces):
+def unpack(n, width, spans, pieces, made):
     share, dtype = pieces[0].shape[1], pieces[0].dtype
     pairs = n // 2
     return pl.pallas_call(
-        functools.partial(unpack_kernel, pairs, width, spans),
+        functools.partial(unpack_kernel, pairs, width, spans, len(made)),
         out_shape=jax.ShapeDtypeStruct((n, share, pairs * width), dtype),
-        in_specs=[ANY] * (pairs * len(spans)),
-        out_specs=ANY,
+        in_specs=[HBM] * len(made) + [ANY] * (pairs * len(spans)),
+        out_specs=HBM,
         scratch_shapes=[pltpu.SemaphoreType.DMA((len(spans), pairs))],
+        input_output_aliases={0: 0} if made else {},
         compiler_params=ROOM,
         name="unpack",
-    )(*pieces)
+    )(*made, *pieces)
 
 
 def swap(x, n, zero, one):
@@ -411,7 +415,12 @@
     spans = [(sum(parts[:c]), count) for c, count in enumerate(parts)]
     arrived = []
     for first, count in spans:
-        pieces = pack(pairs, first, count, plan, docs, q, k, v)
+        order = [pairs // 2, *(k for k in range(pairs) if k != pairs // 2)]
+        cut = pairs if first else 2
+        packed = pack(pairs, first, count, order[:cut], plan, docs, q, k, v)
+        if cut < pairs:
+            packed += pack(pairs, first, count, order[cut:], plan, docs, q, k, v)
+        pieces = [x for _, x in sorted(zip(order, packed), key=lambda pair: pair[0])]
         arrived.append(exchange(n, pieces))
     back, given, marked = [], None, []
     for (first, count), pieces in zip(spans, arrived):
@@ -429,7 +438,10 @@
         if not last:
             marked = [mark(pieces[-1])]
         back += exchange(n, pieces)
-    return unpack(n, width, spans, back).reshape(SPAN, full)
+    made, cut = [], len(spans) - 1
+    if cut:
+        made = [unpack(n, width, spans[:cut], back[: cut * pairs], made)]
+    return unpack(n, width, spans[cut:], back[cut * pairs :], made).reshape(SPAN, full)
 
 
 def solution(mesh):

time: 116 us -> 116 us (level)
  starting transfers between devices: 47.2 us -> 43.8 us
  Pallas kernels: 10.7 us -> 12.6 us
    ppermute x30, starting transfers between devices: 47.2 us -> 43.8 us  [swap(): lax.ppermute(x, AXIS, [(i, i ^ (one if i & 1 else zero)) for i in range(n)])]
    pallas_call x3 -> x5, Pallas kernels: 4.65 us -> 6.55 us  [the longest x3 4.86 us: pack(): pl.pallas_call(functools.partial(pack_kernel, pairs, heads, first, count,...]
  transfers between devices with their start and end apart: 30 -> 30, of which waited for: 14 -> 13; matrix products, arithmetic and copies ran while one was open for 0% -> 0% of each run, Pallas kernels for 6% -> 8%
where the time goes in v1:
time: 116 us; the launch traced here: 114 us
  waiting for transfers between devices  57 us (49%)
  starting transfers between devices  43.8 us (38%)
  Pallas kernels  12.6 us (11%)
    ppermute x30, waiting for transfers between devices, swap(): lax.ppermute(x, AXIS, [(i, i ^ (one if i & 1 else zero)) for i in range(n)])  57 us
    ppermute x30, starting transfers between devices, swap(): lax.ppermute(x, AXIS, [(i, i ^ (one if i & 1 else zero)) for i in range(n)])  43.8 us
    pallas_call x3, Pallas kernels, pack(): pl.pallas_call(functools.partial(pack_kernel, pairs, heads, first, count,...  4.86 us
    pallas_call x2, Pallas kernels, attend(): pl.pallas_call(functools.partial(attend_kernel, pairs, share, width, firs...  4.77 us
  transfers between devices with their start and end apart: 30, of which 13 were waited for; matrix products, arithmetic and copies ran while one was open for 0% of the time, Pallas kernels for 8%

profile of v1, /device:TPU:1, one launch (start us, length us, event | category | flops | bytes accessed | tf_op | source)
XLA Modules:
  0.0 113.6 jit_solution(11818701131080238603)
XLA Ops:
  0.0 1.5 %pack.3 = (bf16[121,8,128]{2,1,0:T(8,128)(2,1)S(1)}, bf16[121,8,128]{2,1,0:T(8,128)(2,1)S(1)}) custom-call(s32[1,128]{1,0:T(1,128)} %plan_ref.5, s32[1,128]{1,0:T(1,128)} %bitcast.23, bf16[16,32,8,128]{3,2,1,0:T(8,128)(2,1)} %bitcast.14, bf16[16,32,8,128]{3,2,1,0:T(8,128)(2,1)} %bitcast.17, bf16[16,32,8,128]{3,2,1,0:T(8,128)(2,1)} %bitcast.20), custom_call_target="tpu_custom_call" | custom-call | tf_op jit(solution)/shard_map/pack/pallas_call | solution.py:190
  1.5 2.1 %collective-permute-start = (bf16[121,8,128]{2,1,0:T(8,128)(2,1)S(1)}, bf16[121,8,128]{2,1,0:T(8,128)(2,1)S(1)}, u32[]{:S(2)}, u32[]{:S(2)}) collective-permute-start(bf16[121,8,128]{2,1,0:T(8,128)(2,1)S(1)} %get-tuple-element.40), channel_id=1, source_target_pairs={{0,14},{1,3},{2,12},{3,1},{4,10},{5,7},{6,8},{7,5},{8,6},{9,11},{1... | collective-permute-start | bytes 743432 | tf_op jit(solution)/shard_map/ppermute | solution.py:395
  3.6 1.8 %pack.4 = (bf16[121,8,128]{2,1,0:T(8,128)(2,1)S(1)}, bf16[121,8,128]{2,1,0:T(8,128)(2,1)S(1)}, bf16[121,8,128]{2,1,0:T(8,128)(2,1)S(1)}, bf16[121,8,128]{2,1,0:T...) custom-call(s32[1,128]{1,0:T(1,128)} %plan_ref.5, s32[1,128]{1,0:T(1,128)} %bitcast.24, ...), custom_call_target="tpu_custom_call" | custom-call | tf_op jit(solution)/shard_map/pack/pallas_call | solution.py:190
  5.4 1.3 %collective-permute-start.1 = (bf16[121,8,128]{2,1,0:T(8,128)(2,1)S(1)}, bf16[121,8,128]{2,1,0:T(8,128)(2,1)S(1)}, u32[]{:S(2)}, u32[]{:S(2)}) collective-permute-start(bf16[121,8,128]{2,1,0:T(8,128)(2,1)S(1)} %get-tuple-element.41), channel_id=1, source_target_pairs={{0,12},{1,7},{2,14},{3,5},{4,8},{5,3},{6,10},{7,1},{8,4},{9,15},{1... | collective-permute-start | bytes 743432 | tf_op jit(solution)/shard_map/ppermute | solution.py:395
  6.8 0.1 collective-permute-start.2
  6.9 4.3 %collective-permute-start.3 = (bf16[121,8,128]{2,1,0:T(8,128)(2,1)S(1)}, bf16[121,8,128]{2,1,0:T(8,128)(2,1)S(1)}, u32[]{:S(2)}, u32[]{:S(2)}) collective-permute-start(bf16[121,8,128]{2,1,0:T(8,128)(2,1)S(1)} %get-tuple-element.43), channel_id=1, source_target_pairs={{0,8},{1,15},{2,10},{3,13},{4,12},{5,11},{6,14},{7,9},{8,0},{9,7},... | collective-permute-start | bytes 743432 | tf_op jit(solution)/shard_map/ppermute | solution.py:395
  11.2 0.0 collective-permute-done.rest_0_.rest_1_
  11.2 5.9 %collective-permute-start.5 = (bf16[121,8,128]{2,1,0:T(8,128)(2,1)S(1)}, bf16[121,8,128]{2,1,0:T(8,128)(2,1)S(1)}, u32[]{:S(2)}, u32[]{:S(2)}) collective-permute-start(bf16[121,8,128]{2,1,0:T(8,128)(2,1)S(1)} %get-tuple-element.45), channel_id=1, source_target_pairs={{0,6},{1,11},{2,4},{3,9},{4,2},{5,15},{6,0},{7,13},{8,14},{9,3},{1... | collective-permute-start | bytes 743432 | tf_op jit(solution)/shard_map/ppermute | solution.py:395
  17.1 0.4 collective-permute-done.2.rest_2_.rest_3_
  17.6 7.7 %collective-permute-done.3.rest_3_.rest_4_ = bf16[121,8,128]{2,1,0:T(8,128)(2,1)S(1)} collective-permute-done((bf16[121,8,128]{2,1,0:T(8,128)(2,1)S(1)}, bf16[121,8,128]{2,1,0:T(8,128)(2,1)S(1)}, u32[]{:S(2)}, u32[]{:S(2)}) %collective-permute-start.3) | collective-permute-done | bytes 247840 | tf_op jit(solution)/shard_map/ppermute | solution.py:395
  25.2 5.3 %collective-permute-done.4.rest_4_.rest_5_ = bf16[121,8,128]{2,1,0:T(8,128)(2,1)S(1)} collective-permute-done((bf16[121,8,128]{2,1,0:T(8,128)(2,1)S(1)}, bf16[121,8,128]{2,1,0:T(8,128)(2,1)S(1)}, u32[]{:S(2)}, u32[]{:S(2)}) %collective-permute-start.4) | collective-permute-done | bytes 247840 | tf_op jit(solution)/shard_map/ppermute | solution.py:395
  30.6 16.0 %collective-permute-done.5.rest_5_.rest_6_ = bf16[121,8,128]{2,1,0:T(8,128)(2,1)S(1)} collective-permute-done((bf16[121,8,128]{2,1,0:T(8,128)(2,1)S(1)}, bf16[121,8,128]{2,1,0:T(8,128)(2,1)S(1)}, u32[]{:S(2)}, u32[]{:S(2)}) %collective-permute-start.5) | collective-permute-done | bytes 247840 | tf_op jit(solution)/shard_map/ppermute | solution.py:395
  46.5 4.0 %collective-permute-done.6.rest_6_.rest_7_ = bf16[121,8,128]{2,1,0:T(8,128)(2,1)S(1)} collective-permute-done((bf16[121,8,128]{2,1,0:T(8,128)(2,1)S(1)}, bf16[121,8,128]{2,1,0:T(8,128)(2,1)S(1)}, u32[]{:S(2)}, u32[]{:S(2)}) %collective-permute-start.6) | collective-permute-done | bytes 247840 | tf_op jit(solution)/shard_map/ppermute | solution.py:395
  50.6 0.5 collect.5.rest_1_
  51.1 1.0 collective-permute-start.7
  52.0 1.6 %pack.5 = (bf16[72,8,128]{2,1,0:T(8,128)(2,1)S(1)}, bf16[72,8,128]{2,1,0:T(8,128)(2,1)S(1)}, bf16[72,8,128]{2,1,0:T(8,128)(2,1)S(1)}, bf16[72,8,128]{2,1,0:T(8,1...) custom-call(s32[1,128]{1,0:T(1,128)} %plan_ref.5, ...), custom_call_target="tpu_custom_call" | custom-call | tf_op jit(solution)/shard_map/pack/pallas_call | solution.py:190
  53.6 0.0 copy-start
  53.6 3.1 %collective-permute-start.15 = (bf16[72,8,128]{2,1,0:T(8,128)(2,1)S(1)}, bf16[72,8,128]{2,1,0:T(8,128)(2,1)S(1)}, u32[]{:S(2)}, u32[]{:S(2)}) collective-permute-start(bf16[72,8,128]{2,1,0:T(8,128)(2,1)S(1)} %get-tuple-element.59), channel_id=1, source_target_pairs={{0,14},{1,3},{2,12},{3,1},{4,10},{5,7},{6,8},{7,5},{8,6},{9,11},{1... | collective-permute-start | bytes 442376 | tf_op jit(solution)/shard_map/ppermute | solution.py:395
  56.7 1.3 %collective-permute-start.17 = (bf16[72,8,128]{2,1,0:T(8,128)(2,1)S(1)}, bf16[72,8,128]{2,1,0:T(8,128)(2,1)S(1)}, u32[]{:S(2)}, u32[]{:S(2)}) collective-permute-start(bf16[72,8,128]{2,1,0:T(8,128)(2,1)S(1)} %get-tuple-element.61), channel_id=1, source_target_pairs={{0,10},{1,5},{2,8},{3,7},{4,14},{5,1},{6,12},{7,3},{8,2},{9,13},{1... | collective-permute-start | bytes 442376 | tf_op jit(solution)/shard_map/ppermute | solution.py:395
  57.9 1.3 %collective-permute-start.18 = (bf16[72,8,128]{2,1,0:T(8,128)(2,1)S(1)}, bf16[72,8,128]{2,1,0:T(8,128)(2,1)S(1)}, u32[]{:S(2)}, u32[]{:S(2)}) collective-permute-start(bf16[72,8,128]{2,1,0:T(8,128)(2,1)S(1)} %get-tuple-element.62), channel_id=1, source_target_pairs={{0,8},{1,15},{2,10},{3,13},{4,12},{5,11},{6,14},{7,9},{8,0},{9,7},... | collective-permute-start | bytes 442376 | tf_op jit(solution)/shard_map/ppermute | solution.py:395
  59.3 1.1 collective-permute-done.15.rest_0_.rest_1_
  60.4 2.0 %collective-permute-start.19 = (bf16[72,8,128]{2,1,0:T(8,128)(2,1)S(1)}, bf16[72,8,128]{2,1,0:T(8,128)(2,1)S(1)}, u32[]{:S(2)}, u32[]{:S(2)}) collective-permute-start(bf16[72,8,128]{2,1,0:T(8,128)(2,1)S(1)} %get-tuple-element.63), channel_id=1, source_target_pairs={{0,2},{1,13},{2,0},{3,15},{4,6},{5,9},{6,4},{7,11},{8,10},{9,5},{1... | collective-permute-start | bytes 442376 | tf_op jit(solution)/shard_map/ppermute | solution.py:395
  62.3 0.9 collective-permute-done.16.rest_1_.rest_2_
  63.2 0.9 collective-permute-start.20
  64.2 0.4 collective-permute-start.21
  64.6 0.3 collect.4.rest_0_
  64.9 2.7 %attend.2 = (bf16[10,8,512]{2,1,0:T(8,128)(2,1)S(1)}, bf16[10,8,512]{2,1,0:T(8,128)(2,1)S(1)}, bf16[10,8,512]{2,1,0:T(8,128)(2,1)S(1)}, bf16[10,8,512]{2,1,0:T(8...) custom-call(f32[32,128]{1,0:T(8,128)S(1)} %bitcast.12, ...), custom_call_target="tpu_custom_call" | custom-call | tf_op jit(solution)/shard_map/attend/pallas_call | solution.py:346
  67.6 2.0 %collective-permute-done.19.rest_4_.rest_5_ = bf16[72,8,128]{2,1,0:T(8,128)(2,1)S(1)} collective-permute-done((bf16[72,8,128]{2,1,0:T(8,128)(2,1)S(1)}, bf16[72,8,128]{2,1,0:T(8,128)(2,1)S(1)}, u32[]{:S(2)}, u32[]{:S(2)}) %collective-permute-start.19) | collective-permute-done | bytes 147488 | tf_op jit(solution)/shard_map/ppermute | solution.py:395
  69.6 11.2 %collective-permute-done.20.rest_5_.rest_6_ = bf16[72,8,128]{2,1,0:T(8,128)(2,1)S(1)} collective-permute-done((bf16[72,8,128]{2,1,0:T(8,128)(2,1)S(1)}, bf16[72,8,128]{2,1,0:T(8,128)(2,1)S(1)}, u32[]{:S(2)}, u32[]{:S(2)}) %collective-permute-start.20) | collective-permute-done | bytes 147488 | tf_op jit(solution)/shard_map/ppermute | solution.py:395
  80.8 3.0 %collective-permute-done.21.rest_6_.rest_7_ = bf16[72,8,128]{2,1,0:T(8,128)(2,1)S(1)} collective-permute-done((bf16[72,8,128]{2,1,0:T(8,128)(2,1)S(1)}, bf16[72,8,128]{2,1,0:T(8,128)(2,1)S(1)}, u32[]{:S(2)}, u32[]{:S(2)}) %collective-permute-start.21) | collective-permute-done | bytes 147488 | tf_op jit(solution)/shard_map/ppermute | solution.py:395
  83.8 0.3 collect.7.rest_4_
  84.1 1.5 %collective-permute-start.22 = (bf16[48,64,128]{2,1,0:T(8,128)(2,1)S(1)}, bf16[48,64,128]{2,1,0:T(8,128)(2,1)S(1)}, u32[]{:S(2)}, u32[]{:S(2)}) collective-permute-start(bf16[48,64,128]{2,1,0:T(8,128)(2,1)S(1)} %collect.7.rest_4_), channel_id=1, source_target_pairs={{0,1},{1,0},{2,3},{3,2},{4,5},{5,4},{6,7},{7,6},{8,9},{9,8},{10,11... | collective-permute-start | bytes 2359304 | tf_op jit(solution)/shard_map/ppermute | solution.py:395
  85.6 0.4 collective-permute-start.9
  86.0 2.2 %collective-permute-start.10 = (bf16[10,8,512]{2,1,0:T(8,128)(2,1)S(1)}, bf16[10,8,512]{2,1,0:T(8,128)(2,1)S(1)}, u32[]{:S(2)}, u32[]{:S(2)}) collective-permute-start(bf16[10,8,512]{2,1,0:T(8,128)(2,1)S(1)} %get-tuple-element.50), channel_id=1, source_target_pairs={{0,10},{1,5},{2,8},{3,7},{4,14},{5,1},{6,12},{7,3},{8,2},{9,13},{1... | collective-permute-start | bytes 245768 | tf_op jit(solution)/shard_map/ppermute | solution.py:395
  88.3 0.6 collective-permute-done.8.rest_0_
  88.9 2.3 %collective-permute-start.12 = (bf16[10,8,512]{2,1,0:T(8,128)(2,1)S(1)}, bf16[10,8,512]{2,1,0:T(8,128)(2,1)S(1)}, u32[]{:S(2)}, u32[]{:S(2)}) collective-permute-start(bf16[10,8,512]{2,1,0:T(8,128)(2,1)S(1)} %get-tuple-element.52), channel_id=1, source_target_pairs={{0,2},{1,13},{2,0},{3,15},{4,6},{5,9},{6,4},{7,11},{8,10},{9,5},{1... | collective-permute-start | bytes 245768 | tf_op jit(solution)/shard_map/ppermute | solution.py:395
  91.2 4.1 %collective-permute-start.14 = (bf16[10,8,512]{2,1,0:T(8,128)(2,1)S(1)}, bf16[10,8,512]{2,1,0:T(8,128)(2,1)S(1)}, u32[]{:S(2)}, u32[]{:S(2)}) collective-permute-start(bf16[10,8,512]{2,1,0:T(8,128)(2,1)S(1)} %get-tuple-element.54), channel_id=1, source_target_pairs={{0,4},{1,9},{2,6},{3,11},{4,0},{5,13},{6,2},{7,15},{8,12},{9,1},{1... | collective-permute-start | bytes 245768 | tf_op jit(solution)/shard_map/ppermute | solution.py:395
  95.4 0.2 collect.6.rest_3_
  95.6 2.1 %attend.3 = (bf16[6,8,512]{2,1,0:T(8,128)(2,1)S(1)}, bf16[6,8,512]{2,1,0:T(8,128)(2,1)S(1)}, bf16[6,8,512]{2,1,0:T(8,128)(2,1)S(1)}, bf16[6,8,512]{2,1,0:T(8,128...) custom-call(f32[32,128]{1,0:T(8,128)S(1)} %bitcast.13, ...), custom_call_target="tpu_custom_call" | custom-call | tf_op jit(solution)/shard_map/attend/pallas_call | solution.py:346
  97.7 0.1 collective-permute-start.23
  97.8 1.8 %collective-permute-start.24 = (bf16[6,8,512]{2,1,0:T(8,128)(2,1)S(1)}, bf16[6,8,512]{2,1,0:T(8,128)(2,1)S(1)}, u32[]{:S(2)}, u32[]{:S(2)}) collective-permute-start(bf16[6,8,512]{2,1,0:T(8,128)(2,1)S(1)} %get-tuple-element.68), channel_id=1, source_target_pairs={{0,12},{1,7},{2,14},{3,5},{4,8},{5,3},{6,10},{7,1},{8,4},{9,15},{1... | collective-permute-start | bytes 147464 | tf_op jit(solution)/shard_map/ppermute | solution.py:395
  99.6 1.0 collective-permute-start.25
  100.6 2.2 %collective-permute-done.13.rest_5_ = bf16[10,8,512]{2,1,0:T(8,128)(2,1)S(1)} collective-permute-done((bf16[10,8,512]{2,1,0:T(8,128)(2,1)S(1)}, bf16[10,8,512]{2,1,0:T(8,128)(2,1)S(1)}, u32[]{:S(2)}, u32[]{:S(2)}) %collective-permute-start.13) | collective-permute-done | bytes 81952 | tf_op jit(solution)/shard_map/ppermute | solution.py:395
  102.8 2.7 %collective-permute-start.27 = (bf16[6,8,512]{2,1,0:T(8,128)(2,1)S(1)}, bf16[6,8,512]{2,1,0:T(8,128)(2,1)S(1)}, u32[]{:S(2)}, u32[]{:S(2)}) collective-permute-start(bf16[6,8,512]{2,1,0:T(8,128)(2,1)S(1)} %get-tuple-element.71), channel_id=1, source_target_pairs={{0,2},{1,13},{2,0},{3,15},{4,6},{5,9},{6,4},{7,11},{8,10},{9,5},{1... | collective-permute-start | bytes 147464 | tf_op jit(solution)/shard_map/ppermute | solution.py:395
  105.4 3.9 %collective-permute-start.29 = (bf16[6,8,512]{2,1,0:T(8,128)(2,1)S(1)}, bf16[6,8,512]{2,1,0:T(8,128)(2,1)S(1)}, u32[]{:S(2)}, u32[]{:S(2)}) collective-permute-start(bf16[6,8,512]{2,1,0:T(8,128)(2,1)S(1)} %get-tuple-element.73), channel_id=1, source_target_pairs={{0,4},{1,9},{2,6},{3,11},{4,0},{5,13},{6,2},{7,15},{8,12},{9,1},{1... | collective-permute-start | bytes 147464 | tf_op jit(solution)/shard_map/ppermute | solution.py:395
  109.3 0.9 unpack.2.rest_0_
  110.2 2.6 %collective-permute-done.28.rest_6_ = bf16[6,8,512]{2,1,0:T(8,128)(2,1)S(1)} collective-permute-done((bf16[6,8,512]{2,1,0:T(8,128)(2,1)S(1)}, bf16[6,8,512]{2,1,0:T(8,128)(2,1)S(1)}, u32[]{:S(2)}, u32[]{:S(2)}) %collective-permute-start.28) | collective-permute-done | bytes 49184 | tf_op jit(solution)/shard_map/ppermute | solution.py:395
  112.8 0.8 unpack.3
  (27 shorter events, 0.1 us)
Async XLA Ops:
  1.5 9.7 %collective-permute-start = (bf16[121,8,128]{2,1,0:T(8,128)(2,1)S(1)}, bf16[121,8,128]{2,1,0:T(8,128)(2,1)S(1)}, u32[]{:S(2)}, u32[]{:S(2)}) collective-permute-start(bf16[121,8,128]{2,1,0:T(8,128)(2,1)S(1)} %get-tuple-element.40), channel_id=1, source_target_pairs={{0,14},{1,3},{2,12},{3,1},{4,10},{5,7},{6,8},{7,5},{8,6},{9,11},{1... | collective-permute-start | bytes 743432 | tf_op jit(solution)/shard_map/ppermute | solution.py:395
  5.4 11.7 %collective-permute-start.1 = (bf16[121,8,128]{2,1,0:T(8,128)(2,1)S(1)}, bf16[121,8,128]{2,1,0:T(8,128)(2,1)S(1)}, u32[]{:S(2)}, u32[]{:S(2)}) collective-permute-start(bf16[121,8,128]{2,1,0:T(8,128)(2,1)S(1)} %get-tuple-element.41), channel_id=1, source_target_pairs={{0,12},{1,7},{2,14},{3,5},{4,8},{5,3},{6,10},{7,1},{8,4},{9,15},{1... | collective-permute-start | bytes 743432 | tf_op jit(solution)/shard_map/ppermute | solution.py:395
  6.8 10.8 %collective-permute-start.2 = (bf16[121,8,128]{2,1,0:T(8,128)(2,1)S(1)}, bf16[121,8,128]{2,1,0:T(8,128)(2,1)S(1)}, u32[]{:S(2)}, u32[]{:S(2)}) collective-permute-start(bf16[121,8,128]{2,1,0:T(8,128)(2,1)S(1)} %get-tuple-element.42), channel_id=1, source_target_pairs={{0,10},{1,5},{2,8},{3,7},{4,14},{5,1},{6,12},{7,3},{8,2},{9,13},{1... | collective-permute-start | bytes 743432 | tf_op jit(solution)/shard_map/ppermute | solution.py:395
  6.9 18.3 %collective-permute-start.3 = (bf16[121,8,128]{2,1,0:T(8,128)(2,1)S(1)}, bf16[121,8,128]{2,1,0:T(8,128)(2,1)S(1)}, u32[]{:S(2)}, u32[]{:S(2)}) collective-permute-start(bf16[121,8,128]{2,1,0:T(8,128)(2,1)S(1)} %get-tuple-element.43), channel_id=1, source_target_pairs={{0,8},{1,15},{2,10},{3,13},{4,12},{5,11},{6,14},{7,9},{8,0},{9,7},... | collective-permute-start | bytes 743432 | tf_op jit(solution)/shard_map/ppermute | solution.py:395
  11.2 19.4 %collective-permute-start.4 = (bf16[121,8,128]{2,1,0:T(8,128)(2,1)S(1)}, bf16[121,8,128]{2,1,0:T(8,128)(2,1)S(1)}, u32[]{:S(2)}, u32[]{:S(2)}) collective-permute-start(bf16[121,8,128]{2,1,0:T(8,128)(2,1)S(1)} %get-tuple-element.44), channel_id=1, source_target_pairs={{0,2},{1,13},{2,0},{3,15},{4,6},{5,9},{6,4},{7,11},{8,10},{9,5},{1... | collective-permute-start | bytes 743432 | tf_op jit(solution)/shard_map/ppermute | solution.py:395
  11.2 35.3 %collective-permute-start.5 = (bf16[121,8,128]{2,1,0:T(8,128)(2,1)S(1)}, bf16[121,8,128]{2,1,0:T(8,128)(2,1)S(1)}, u32[]{:S(2)}, u32[]{:S(2)}) collective-permute-start(bf16[121,8,128]{2,1,0:T(8,128)(2,1)S(1)} %get-tuple-element.45), channel_id=1, source_target_pairs={{0,6},{1,11},{2,4},{3,9},{4,2},{5,15},{6,0},{7,13},{8,14},{9,3},{1... | collective-permute-start | bytes 743432 | tf_op jit(solution)/shard_map/ppermute | solution.py:395
  17.1 33.4 %collective-permute-start.6 = (bf16[121,8,128]{2,1,0:T(8,128)(2,1)S(1)}, bf16[121,8,128]{2,1,0:T(8,128)(2,1)S(1)}, u32[]{:S(2)}, u32[]{:S(2)}) collective-permute-start(bf16[121,8,128]{2,1,0:T(8,128)(2,1)S(1)} %get-tuple-element.46), channel_id=1, source_target_pairs={{0,4},{1,9},{2,6},{3,11},{4,0},{5,13},{6,2},{7,15},{8,12},{9,1},{1... | collective-permute-start | bytes 743432 | tf_op jit(solution)/shard_map/ppermute | solution.py:395
  51.1 13.1 %collective-permute-start.7 = (bf16[81,64,128]{2,1,0:T(8,128)(2,1)S(1)}, bf16[81,64,128]{2,1,0:T(8,128)(2,1)S(1)}, u32[]{:S(2)}, u32[]{:S(2)}) collective-permute-start(bf16[81,64,128]{2,1,0:T(8,128)(2,1)S(1)} %collect.5.rest_1_), channel_id=1, source_target_pairs={{0,1},{1,0},{2,3},{3,2},{4,5},{5,4},{6,7},{7,6},{8,9},{9,8},{10,11... | collective-permute-start | bytes 3981320 | tf_op jit(solution)/shard_map/ppermute | solution.py:395
  53.6 11.3 %copy-start = (f32[4096]{0:T(1024)S(1)}, f32[4096]{0:T(1024)}, u32[]{:S(2)}) copy-start(f32[4096]{0:T(1024)} %param.11) | copy-start | bytes 49156
  53.6 6.8 %collective-permute-start.15 = (bf16[72,8,128]{2,1,0:T(8,128)(2,1)S(1)}, bf16[72,8,128]{2,1,0:T(8,128)(2,1)S(1)}, u32[]{:S(2)}, u32[]{:S(2)}) collective-permute-start(bf16[72,8,128]{2,1,0:T(8,128)(2,1)S(1)} %get-tuple-element.59), channel_id=1, source_target_pairs={{0,14},{1,3},{2,12},{3,1},{4,10},{5,7},{6,8},{7,5},{8,6},{9,11},{1... | collective-permute-start | bytes 442376 | tf_op jit(solution)/shard_map/ppermute | solution.py:395
  56.7 6.5 %collective-permute-start.16 = (bf16[72,8,128]{2,1,0:T(8,128)(2,1)S(1)}, bf16[72,8,128]{2,1,0:T(8,128)(2,1)S(1)}, u32[]{:S(2)}, u32[]{:S(2)}) collective-permute-start(bf16[72,8,128]{2,1,0:T(8,128)(2,1)S(1)} %get-tuple-element.60), channel_id=1, source_target_pairs={{0,12},{1,7},{2,14},{3,5},{4,8},{5,3},{6,10},{7,1},{8,4},{9,15},{1... | collective-permute-start | bytes 442376 | tf_op jit(solution)/shard_map/ppermute | solution.py:395
  56.7 10.9 %collective-permute-start.17 = (bf16[72,8,128]{2,1,0:T(8,128)(2,1)S(1)}, bf16[72,8,128]{2,1,0:T(8,128)(2,1)S(1)}, u32[]{:S(2)}, u32[]{:S(2)}) collective-permute-start(bf16[72,8,128]{2,1,0:T(8,128)(2,1)S(1)} %get-tuple-element.61), channel_id=1, source_target_pairs={{0,10},{1,5},{2,8},{3,7},{4,14},{5,1},{6,12},{7,3},{8,2},{9,13},{1... | collective-permute-start | bytes 442376 | tf_op jit(solution)/shard_map/ppermute | solution.py:395
  57.9 9.7 %collective-permute-start.18 = (bf16[72,8,128]{2,1,0:T(8,128)(2,1)S(1)}, bf16[72,8,128]{2,1,0:T(8,128)(2,1)S(1)}, u32[]{:S(2)}, u32[]{:S(2)}) collective-permute-start(bf16[72,8,128]{2,1,0:T(8,128)(2,1)S(1)} %get-tuple-element.62), channel_id=1, source_target_pairs={{0,8},{1,15},{2,10},{3,13},{4,12},{5,11},{6,14},{7,9},{8,0},{9,7},... | collective-permute-start | bytes 442376 | tf_op jit(solution)/shard_map/ppermute | solution.py:395
  60.4 9.3 %collective-permute-start.19 = (bf16[72,8,128]{2,1,0:T(8,128)(2,1)S(1)}, bf16[72,8,128]{2,1,0:T(8,128)(2,1)S(1)}, u32[]{:S(2)}, u32[]{:S(2)}) collective-permute-start(bf16[72,8,128]{2,1,0:T(8,128)(2,1)S(1)} %get-tuple-element.63), channel_id=1, source_target_pairs={{0,2},{1,13},{2,0},{3,15},{4,6},{5,9},{6,4},{7,11},{8,10},{9,5},{1... | collective-permute-start | bytes 442376 | tf_op jit(solution)/shard_map/ppermute | solution.py:395
  63.2 17.6 %collective-permute-start.20 = (bf16[72,8,128]{2,1,0:T(8,128)(2,1)S(1)}, bf16[72,8,128]{2,1,0:T(8,128)(2,1)S(1)}, u32[]{:S(2)}, u32[]{:S(2)}) collective-permute-start(bf16[72,8,128]{2,1,0:T(8,128)(2,1)S(1)} %get-tuple-element.64), channel_id=1, source_target_pairs={{0,6},{1,11},{2,4},{3,9},{4,2},{5,15},{6,0},{7,13},{8,14},{9,3},{1... | collective-permute-start | bytes 442376 | tf_op jit(solution)/shard_map/ppermute | solution.py:395
  64.2 19.7 %collective-permute-start.21 = (bf16[72,8,128]{2,1,0:T(8,128)(2,1)S(1)}, bf16[72,8,128]{2,1,0:T(8,128)(2,1)S(1)}, u32[]{:S(2)}, u32[]{:S(2)}) collective-permute-start(bf16[72,8,128]{2,1,0:T(8,128)(2,1)S(1)} %get-tuple-element.65), channel_id=1, source_target_pairs={{0,4},{1,9},{2,6},{3,11},{4,0},{5,13},{6,2},{7,15},{8,12},{9,1},{1... | collective-permute-start | bytes 442376 | tf_op jit(solution)/shard_map/ppermute | solution.py:395
  84.1 7.1 %collective-permute-start.22 = (bf16[48,64,128]{2,1,0:T(8,128)(2,1)S(1)}, bf16[48,64,128]{2,1,0:T(8,128)(2,1)S(1)}, u32[]{:S(2)}, u32[]{:S(2)}) collective-permute-start(bf16[48,64,128]{2,1,0:T(8,128)(2,1)S(1)} %collect.7.rest_4_), channel_id=1, source_target_pairs={{0,1},{1,0},{2,3},{3,2},{4,5},{5,4},{6,7},{7,6},{8,9},{9,8},{10,11... | collective-permute-start | bytes 2359304 | tf_op jit(solution)/shard_map/ppermute | solution.py:395
  85.6 3.3 %collective-permute-start.8 = (bf16[10,8,512]{2,1,0:T(8,128)(2,1)S(1)}, bf16[10,8,512]{2,1,0:T(8,128)(2,1)S(1)}, u32[]{:S(2)}, u32[]{:S(2)}) collective-permute-start(bf16[10,8,512]{2,1,0:T(8,128)(2,1)S(1)} %get-tuple-element.48), channel_id=1, source_target_pairs={{0,14},{1,3},{2,12},{3,1},{4,10},{5,7},{6,8},{7,5},{8,6},{9,11},{1... | collective-permute-start | bytes 245768 | tf_op jit(solution)/shard_map/ppermute | solution.py:395
  85.6 5.6 %collective-permute-start.9 = (bf16[10,8,512]{2,1,0:T(8,128)(2,1)S(1)}, bf16[10,8,512]{2,1,0:T(8,128)(2,1)S(1)}, u32[]{:S(2)}, u32[]{:S(2)}) collective-permute-start(bf16[10,8,512]{2,1,0:T(8,128)(2,1)S(1)} %get-tuple-element.49), channel_id=1, source_target_pairs={{0,12},{1,7},{2,14},{3,5},{4,8},{5,3},{6,10},{7,1},{8,4},{9,15},{1... | collective-permute-start | bytes 245768 | tf_op jit(solution)/shard_map/ppermute | solution.py:395
  86.0 11.6 %collective-permute-start.10 = (bf16[10,8,512]{2,1,0:T(8,128)(2,1)S(1)}, bf16[10,8,512]{2,1,0:T(8,128)(2,1)S(1)}, u32[]{:S(2)}, u32[]{:S(2)}) collective-permute-start(bf16[10,8,512]{2,1,0:T(8,128)(2,1)S(1)} %get-tuple-element.50), channel_id=1, source_target_pairs={{0,10},{1,5},{2,8},{3,7},{4,14},{5,1},{6,12},{7,3},{8,2},{9,13},{1... | collective-permute-start | bytes 245768 | tf_op jit(solution)/shard_map/ppermute | solution.py:395
  88.2 9.5 %collective-permute-start.11 = (bf16[10,8,512]{2,1,0:T(8,128)(2,1)S(1)}, bf16[10,8,512]{2,1,0:T(8,128)(2,1)S(1)}, u32[]{:S(2)}, u32[]{:S(2)}) collective-permute-start(bf16[10,8,512]{2,1,0:T(8,128)(2,1)S(1)} %get-tuple-element.51), channel_id=1, source_target_pairs={{0,8},{1,15},{2,10},{3,13},{4,12},{5,11},{6,14},{7,9},{8,0},{9,7},... | collective-permute-start | bytes 245768 | tf_op jit(solution)/shard_map/ppermute | solution.py:395
  88.9 10.7 %collective-permute-start.12 = (bf16[10,8,512]{2,1,0:T(8,128)(2,1)S(1)}, bf16[10,8,512]{2,1,0:T(8,128)(2,1)S(1)}, u32[]{:S(2)}, u32[]{:S(2)}) collective-permute-start(bf16[10,8,512]{2,1,0:T(8,128)(2,1)S(1)} %get-tuple-element.52), channel_id=1, source_target_pairs={{0,2},{1,13},{2,0},{3,15},{4,6},{5,9},{6,4},{7,11},{8,10},{9,5},{1... | collective-permute-start | bytes 245768 | tf_op jit(solution)/shard_map/ppermute | solution.py:395
  91.2 11.5 %collective-permute-start.13 = (bf16[10,8,512]{2,1,0:T(8,128)(2,1)S(1)}, bf16[10,8,512]{2,1,0:T(8,128)(2,1)S(1)}, u32[]{:S(2)}, u32[]{:S(2)}) collective-permute-start(bf16[10,8,512]{2,1,0:T(8,128)(2,1)S(1)} %get-tuple-element.53), channel_id=1, source_target_pairs={{0,6},{1,11},{2,4},{3,9},{4,2},{5,15},{6,0},{7,13},{8,14},{9,3},{1... | collective-permute-start | bytes 245768 | tf_op jit(solution)/shard_map/ppermute | solution.py:395
  91.2 11.5 %collective-permute-start.14 = (bf16[10,8,512]{2,1,0:T(8,128)(2,1)S(1)}, bf16[10,8,512]{2,1,0:T(8,128)(2,1)S(1)}, u32[]{:S(2)}, u32[]{:S(2)}) collective-permute-start(bf16[10,8,512]{2,1,0:T(8,128)(2,1)S(1)} %get-tuple-element.54), channel_id=1, source_target_pairs={{0,4},{1,9},{2,6},{3,11},{4,0},{5,13},{6,2},{7,15},{8,12},{9,1},{1... | collective-permute-start | bytes 245768 | tf_op jit(solution)/shard_map/ppermute | solution.py:395
  97.7 7.7 %collective-permute-start.23 = (bf16[6,8,512]{2,1,0:T(8,128)(2,1)S(1)}, bf16[6,8,512]{2,1,0:T(8,128)(2,1)S(1)}, u32[]{:S(2)}, u32[]{:S(2)}) collective-permute-start(bf16[6,8,512]{2,1,0:T(8,128)(2,1)S(1)} %get-tuple-element.67), channel_id=1, source_target_pairs={{0,14},{1,3},{2,12},{3,1},{4,10},{5,7},{6,8},{7,5},{8,6},{9,11},{1... | collective-permute-start | bytes 147464 | tf_op jit(solution)/shard_map/ppermute | solution.py:395
  97.8 7.6 %collective-permute-start.24 = (bf16[6,8,512]{2,1,0:T(8,128)(2,1)S(1)}, bf16[6,8,512]{2,1,0:T(8,128)(2,1)S(1)}, u32[]{:S(2)}, u32[]{:S(2)}) collective-permute-start(bf16[6,8,512]{2,1,0:T(8,128)(2,1)S(1)} %get-tuple-element.68), channel_id=1, source_target_pairs={{0,12},{1,7},{2,14},{3,5},{4,8},{5,3},{6,10},{7,1},{8,4},{9,15},{1... | collective-permute-start | bytes 147464 | tf_op jit(solution)/shard_map/ppermute | solution.py:395
  99.6 10.6 %collective-permute-start.25 = (bf16[6,8,512]{2,1,0:T(8,128)(2,1)S(1)}, bf16[6,8,512]{2,1,0:T(8,128)(2,1)S(1)}, u32[]{:S(2)}, u32[]{:S(2)}) collective-permute-start(bf16[6,8,512]{2,1,0:T(8,128)(2,1)S(1)} %get-tuple-element.69), channel_id=1, source_target_pairs={{0,10},{1,5},{2,8},{3,7},{4,14},{5,1},{6,12},{7,3},{8,2},{9,13},{1... | collective-permute-start | bytes 147464 | tf_op jit(solution)/shard_map/ppermute | solution.py:395
  102.8 7.5 %collective-permute-start.26 = (bf16[6,8,512]{2,1,0:T(8,128)(2,1)S(1)}, bf16[6,8,512]{2,1,0:T(8,128)(2,1)S(1)}, u32[]{:S(2)}, u32[]{:S(2)}) collective-permute-start(bf16[6,8,512]{2,1,0:T(8,128)(2,1)S(1)} %get-tuple-element.70), channel_id=1, source_target_pairs={{0,8},{1,15},{2,10},{3,13},{4,12},{5,11},{6,14},{7,9},{8,0},{9,7},... | collective-permute-start | bytes 147464 | tf_op jit(solution)/shard_map/ppermute | solution.py:395
  102.8 7.5 %collective-permute-start.27 = (bf16[6,8,512]{2,1,0:T(8,128)(2,1)S(1)}, bf16[6,8,512]{2,1,0:T(8,128)(2,1)S(1)}, u32[]{:S(2)}, u32[]{:S(2)}) collective-permute-start(bf16[6,8,512]{2,1,0:T(8,128)(2,1)S(1)} %get-tuple-element.71), channel_id=1, source_target_pairs={{0,2},{1,13},{2,0},{3,15},{4,6},{5,9},{6,4},{7,11},{8,10},{9,5},{1... | collective-permute-start | bytes 147464 | tf_op jit(solution)/shard_map/ppermute | solution.py:395
  105.4 7.4 %collective-permute-start.28 = (bf16[6,8,512]{2,1,0:T(8,128)(2,1)S(1)}, bf16[6,8,512]{2,1,0:T(8,128)(2,1)S(1)}, u32[]{:S(2)}, u32[]{:S(2)}) collective-permute-start(bf16[6,8,512]{2,1,0:T(8,128)(2,1)S(1)} %get-tuple-element.72), channel_id=1, source_target_pairs={{0,6},{1,11},{2,4},{3,9},{4,2},{5,15},{6,0},{7,13},{8,14},{9,3},{1... | collective-permute-start | bytes 147464 | tf_op jit(solution)/shard_map/ppermute | solution.py:395
  105.4 7.4 %collective-permute-start.29 = (bf16[6,8,512]{2,1,0:T(8,128)(2,1)S(1)}, bf16[6,8,512]{2,1,0:T(8,128)(2,1)S(1)}, u32[]{:S(2)}, u32[]{:S(2)}) collective-permute-start(bf16[6,8,512]{2,1,0:T(8,128)(2,1)S(1)} %get-tuple-element.73), channel_id=1, source_target_pairs={{0,4},{1,9},{2,6},{3,11},{4,0},{5,13},{6,2},{7,15},{8,12},{9,1},{1... | collective-permute-start | bytes 147464 | tf_op jit(solution)/shard_map/ppermute | solution.py:395

commit v2 on v1

--- a/solution.py
+++ b/solution.py
@@ -99,9 +99,14 @@
 
 
 def slots(pairs):
-    far = list(range(pairs - 1, pairs // 2 - 1, -1))
+    half, most = pairs // 2, 3 * pairs // 4
+    far = [*range(most - 1, half - 1, -1), *range(pairs - 1, most - 1, -1)]
     near = [1, *range(pairs // 2 - 1, 1, -1)]
-    return list(zip(far + near, near + far)) + [(0, 0)]
+    return list(zip(far + near, near + sorted(far, reverse=True))) + [(0, 0)]
+
+
+def early_slot(pairs):
+    return min(pairs // 2 + 1, pairs - 2)
 
 
 def place():
@@ -415,7 +420,7 @@
     spans = [(sum(parts[:c]), count) for c, count in enumerate(parts)]
     arrived = []
     for first, count in spans:
-        order = [pairs // 2, *(k for k in range(pairs) if k != pairs // 2)]
+        order = sorted(range(pairs), key=lambda k: (k != early_slot(pairs), k))
         cut = pairs if first else 2
         packed = pack(pairs, first, count, order[:cut], plan, docs, q, k, v)
         if cut < pairs:

time: 116 us -> 120 us (1.034)
  the two profiles are of different devices: /device:TPU:1 before, /device:TPU:0 now
where the time goes in v2:
time: 120 us
  starting transfers between devices  53.7 us (45%)
  waiting for transfers between devices  53 us (44%)
  Pallas kernels  12.6 us (10%)
    ppermute x30, starting transfers between devices, swap(): lax.ppermute(x, AXIS, [(i, i ^ (one if i & 1 else zero)) for i in range(n)])  53.7 us
    ppermute x30, waiting for transfers between devices, swap(): lax.ppermute(x, AXIS, [(i, i ^ (one if i & 1 else zero)) for i in range(n)])  53 us
    pallas_call x3, Pallas kernels, pack(): pl.pallas_call(functools.partial(pack_kernel, pairs, heads, first, count,...  4.86 us
    pallas_call x2, Pallas kernels, attend(): pl.pallas_call(functools.partial(attend_kernel, pairs, share, width, firs...  4.76 us
  transfers between devices with their start and end apart: 30, of which 12 were waited for; matrix products, arithmetic and copies ran while one was open for 0% of the time, Pallas kernels for 8%

profile of v2, /device:TPU:0, one launch (start us, length us, event | category | flops | bytes accessed | tf_op | source)
XLA Modules:
  0.0 119.6 jit_solution(8153569209691388120)
XLA Ops:
  0.0 1.5 %pack.3 = (bf16[121,8,128]{2,1,0:T(8,128)(2,1)S(1)}, bf16[121,8,128]{2,1,0:T(8,128)(2,1)S(1)}) custom-call(s32[1,128]{1,0:T(1,128)} %plan_ref.5, s32[1,128]{1,0:T(1,128)} %bitcast.23, bf16[16,32,8,128]{3,2,1,0:T(8,128)(2,1)} %bitcast.14, bf16[16,32,8,128]{3,2,1,0:T(8,128)(2,1)} %bitcast.17, bf16[16,32,8,128]{3,2,1,0:T(8,128)(2,1)} %bitcast.20), custom_call_target="tpu_custom_call" | custom-call | tf_op jit(solution)/shard_map/pack/pallas_call | solution.py:195
  1.5 5.1 %collective-permute-start = (bf16[121,8,128]{2,1,0:T(8,128)(2,1)S(1)}, bf16[121,8,128]{2,1,0:T(8,128)(2,1)S(1)}, u32[]{:S(2)}, u32[]{:S(2)}) collective-permute-start(bf16[121,8,128]{2,1,0:T(8,128)(2,1)S(1)} %get-tuple-element.40), channel_id=1, source_target_pairs={{0,10},{1,3},{2,8},{3,1},{4,14},{5,7},{6,12},{7,5},{8,2},{9,11},{1... | collective-permute-start | bytes 743432 | tf_op jit(solution)/shard_map/ppermute | solution.py:400
  6.6 1.8 %pack.4 = (bf16[121,8,128]{2,1,0:T(8,128)(2,1)S(1)}, bf16[121,8,128]{2,1,0:T(8,128)(2,1)S(1)}, bf16[121,8,128]{2,1,0:T(8,128)(2,1)S(1)}, bf16[121,8,128]{2,1,0:T...) custom-call(s32[1,128]{1,0:T(1,128)} %plan_ref.5, s32[1,128]{1,0:T(1,128)} %bitcast.24, ...), custom_call_target="tpu_custom_call" | custom-call | tf_op jit(solution)/shard_map/pack/pallas_call | solution.py:195
  8.4 0.4 collective-permute-start.1
  8.8 3.5 %collective-permute-start.2 = (bf16[121,8,128]{2,1,0:T(8,128)(2,1)S(1)}, bf16[121,8,128]{2,1,0:T(8,128)(2,1)S(1)}, u32[]{:S(2)}, u32[]{:S(2)}) collective-permute-start(bf16[121,8,128]{2,1,0:T(8,128)(2,1)S(1)} %get-tuple-element.42), channel_id=1, source_target_pairs={{0,14},{1,5},{2,12},{3,7},{4,10},{5,1},{6,8},{7,3},{8,6},{9,13},{1... | collective-permute-start | bytes 743432 | tf_op jit(solution)/shard_map/ppermute | solution.py:400
  12.4 1.7 %collective-permute-start.4 = (bf16[121,8,128]{2,1,0:T(8,128)(2,1)S(1)}, bf16[121,8,128]{2,1,0:T(8,128)(2,1)S(1)}, u32[]{:S(2)}, u32[]{:S(2)}) collective-permute-start(bf16[121,8,128]{2,1,0:T(8,128)(2,1)S(1)} %get-tuple-element.44), channel_id=1, source_target_pairs={{0,2},{1,13},{2,0},{3,15},{4,6},{5,9},{6,4},{7,11},{8,10},{9,5},{1... | collective-permute-start | bytes 743432 | tf_op jit(solution)/shard_map/ppermute | solution.py:400
  14.1 1.2 collective-permute-done.rest_0_.rest_1_
  15.3 3.7 %collective-permute-start.5 = (bf16[121,8,128]{2,1,0:T(8,128)(2,1)S(1)}, bf16[121,8,128]{2,1,0:T(8,128)(2,1)S(1)}, u32[]{:S(2)}, u32[]{:S(2)}) collective-permute-start(bf16[121,8,128]{2,1,0:T(8,128)(2,1)S(1)} %get-tuple-element.45), channel_id=1, source_target_pairs={{0,6},{1,11},{2,4},{3,9},{4,2},{5,15},{6,0},{7,13},{8,14},{9,3},{1... | collective-permute-start | bytes 743432 | tf_op jit(solution)/shard_map/ppermute | solution.py:400
  19.0 19.9 %collective-permute-done.1.rest_1_.rest_2_ = bf16[121,8,128]{2,1,0:T(8,128)(2,1)S(1)} collective-permute-done((bf16[121,8,128]{2,1,0:T(8,128)(2,1)S(1)}, bf16[121,8,128]{2,1,0:T(8,128)(2,1)S(1)}, u32[]{:S(2)}, u32[]{:S(2)}) %collective-permute-start.1) | collective-permute-done | bytes 247840 | tf_op jit(solution)/shard_map/ppermute | solution.py:400
  38.9 1.2 %collective-permute-start.6 = (bf16[121,8,128]{2,1,0:T(8,128)(2,1)S(1)}, bf16[121,8,128]{2,1,0:T(8,128)(2,1)S(1)}, u32[]{:S(2)}, u32[]{:S(2)}) collective-permute-start(bf16[121,8,128]{2,1,0:T(8,128)(2,1)S(1)} %get-tuple-element.46), channel_id=1, source_target_pairs={{0,4},{1,9},{2,6},{3,11},{4,0},{5,13},{6,2},{7,15},{8,12},{9,1},{1... | collective-permute-start | bytes 743432 | tf_op jit(solution)/shard_map/ppermute | solution.py:400
  40.1 7.6 %collective-permute-done.6.rest_6_.rest_7_ = bf16[121,8,128]{2,1,0:T(8,128)(2,1)S(1)} collective-permute-done((bf16[121,8,128]{2,1,0:T(8,128)(2,1)S(1)}, bf16[121,8,128]{2,1,0:T(8,128)(2,1)S(1)}, u32[]{:S(2)}, u32[]{:S(2)}) %collective-permute-start.6) | collective-permute-done | bytes 247840 | tf_op jit(solution)/shard_map/ppermute | solution.py:400
  47.8 0.5 collect.5.rest_1_
  48.3 3.4 %collective-permute-start.7 = (bf16[81,64,128]{2,1,0:T(8,128)(2,1)S(1)}, bf16[81,64,128]{2,1,0:T(8,128)(2,1)S(1)}, u32[]{:S(2)}, u32[]{:S(2)}) collective-permute-start(bf16[81,64,128]{2,1,0:T(8,128)(2,1)S(1)} %collect.5.rest_1_), channel_id=1, source_target_pairs={{0,1},{1,0},{2,3},{3,2},{4,5},{5,4},{6,7},{7,6},{8,9},{9,8},{10,11... | collective-permute-start | bytes 3981320 | tf_op jit(solution)/shard_map/ppermute | solution.py:400
  51.7 1.6 %pack.5 = (bf16[72,8,128]{2,1,0:T(8,128)(2,1)S(1)}, bf16[72,8,128]{2,1,0:T(8,128)(2,1)S(1)}, bf16[72,8,128]{2,1,0:T(8,128)(2,1)S(1)}, bf16[72,8,128]{2,1,0:T(8,1...) custom-call(s32[1,128]{1,0:T(1,128)} %plan_ref.5, ...), custom_call_target="tpu_custom_call" | custom-call | tf_op jit(solution)/shard_map/pack/pallas_call | solution.py:195
  53.2 1.9 %collective-permute-start.15 = (bf16[72,8,128]{2,1,0:T(8,128)(2,1)S(1)}, bf16[72,8,128]{2,1,0:T(8,128)(2,1)S(1)}, u32[]{:S(2)}, u32[]{:S(2)}) collective-permute-start(bf16[72,8,128]{2,1,0:T(8,128)(2,1)S(1)} %get-tuple-element.59), channel_id=1, source_target_pairs={{0,10},{1,3},{2,8},{3,1},{4,14},{5,7},{6,12},{7,5},{8,2},{9,11},{1... | collective-permute-start | bytes 442376 | tf_op jit(solution)/shard_map/ppermute | solution.py:400
  55.1 0.5 collective-permute-start.16
  55.6 5.0 %collective-permute-start.17 = (bf16[72,8,128]{2,1,0:T(8,128)(2,1)S(1)}, bf16[72,8,128]{2,1,0:T(8,128)(2,1)S(1)}, u32[]{:S(2)}, u32[]{:S(2)}) collective-permute-start(bf16[72,8,128]{2,1,0:T(8,128)(2,1)S(1)} %get-tuple-element.61), channel_id=1, source_target_pairs={{0,14},{1,5},{2,12},{3,7},{4,10},{5,1},{6,8},{7,3},{8,6},{9,13},{1... | collective-permute-start | bytes 442376 | tf_op jit(solution)/shard_map/ppermute | solution.py:400
  60.6 0.3 collective-permute-start.18
  61.0 2.0 %collective-permute-done.15.rest_0_.rest_1_ = bf16[72,8,128]{2,1,0:T(8,128)(2,1)S(1)} collective-permute-done((bf16[72,8,128]{2,1,0:T(8,128)(2,1)S(1)}, bf16[72,8,128]{2,1,0:T(8,128)(2,1)S(1)}, u32[]{:S(2)}, u32[]{:S(2)}) %collective-permute-start.15) | collective-permute-done | bytes 147488 | tf_op jit(solution)/shard_map/ppermute | solution.py:400
  63.0 11.7 %collective-permute-done.16.rest_1_.rest_2_ = bf16[72,8,128]{2,1,0:T(8,128)(2,1)S(1)} collective-permute-done((bf16[72,8,128]{2,1,0:T(8,128)(2,1)S(1)}, bf16[72,8,128]{2,1,0:T(8,128)(2,1)S(1)}, u32[]{:S(2)}, u32[]{:S(2)}) %collective-permute-start.16) | collective-permute-done | bytes 147488 | tf_op jit(solution)/shard_map/ppermute | solution.py:400
  74.7 2.8 %collective-permute-start.20 = (bf16[72,8,128]{2,1,0:T(8,128)(2,1)S(1)}, bf16[72,8,128]{2,1,0:T(8,128)(2,1)S(1)}, u32[]{:S(2)}, u32[]{:S(2)}) collective-permute-start(bf16[72,8,128]{2,1,0:T(8,128)(2,1)S(1)} %get-tuple-element.64), channel_id=1, source_target_pairs={{0,6},{1,11},{2,4},{3,9},{4,2},{5,15},{6,0},{7,13},{8,14},{9,3},{1... | collective-permute-start | bytes 442376 | tf_op jit(solution)/shard_map/ppermute | solution.py:400
  77.5 1.3 %collective-permute-start.21 = (bf16[72,8,128]{2,1,0:T(8,128)(2,1)S(1)}, bf16[72,8,128]{2,1,0:T(8,128)(2,1)S(1)}, u32[]{:S(2)}, u32[]{:S(2)}) collective-permute-start(bf16[72,8,128]{2,1,0:T(8,128)(2,1)S(1)} %get-tuple-element.65), channel_id=1, source_target_pairs={{0,4},{1,9},{2,6},{3,11},{4,0},{5,13},{6,2},{7,15},{8,12},{9,1},{1... | collective-permute-start | bytes 442376 | tf_op jit(solution)/shard_map/ppermute | solution.py:400
  78.9 0.3 collect.4.rest_0_
  79.2 2.7 %attend.2 = (bf16[10,8,512]{2,1,0:T(8,128)(2,1)S(1)}, bf16[10,8,512]{2,1,0:T(8,128)(2,1)S(1)}, bf16[10,8,512]{2,1,0:T(8,128)(2,1)S(1)}, bf16[10,8,512]{2,1,0:T(8...) custom-call(f32[32,128]{1,0:T(8,128)S(1)} %bitcast.12, ...), custom_call_target="tpu_custom_call" | custom-call | tf_op jit(solution)/shard_map/attend/pallas_call | solution.py:351
  81.9 0.5 collective-permute-done.20.rest_5_.rest_6_
  82.3 2.9 %collective-permute-done.21.rest_6_.rest_7_ = bf16[72,8,128]{2,1,0:T(8,128)(2,1)S(1)} collective-permute-done((bf16[72,8,128]{2,1,0:T(8,128)(2,1)S(1)}, bf16[72,8,128]{2,1,0:T(8,128)(2,1)S(1)}, u32[]{:S(2)}, u32[]{:S(2)}) %collective-permute-start.21) | collective-permute-done | bytes 147488 | tf_op jit(solution)/shard_map/ppermute | solution.py:400
  85.3 0.3 collect.7.rest_4_
  85.7 1.5 %collective-permute-start.8 = (bf16[10,8,512]{2,1,0:T(8,128)(2,1)S(1)}, bf16[10,8,512]{2,1,0:T(8,128)(2,1)S(1)}, u32[]{:S(2)}, u32[]{:S(2)}) collective-permute-start(bf16[10,8,512]{2,1,0:T(8,128)(2,1)S(1)} %get-tuple-element.48), channel_id=1, source_target_pairs={{0,10},{1,3},{2,8},{3,1},{4,14},{5,7},{6,12},{7,5},{8,2},{9,11},{1... | collective-permute-start | bytes 245768 | tf_op jit(solution)/shard_map/ppermute | solution.py:400
  87.2 1.3 %collective-permute-start.9 = (bf16[10,8,512]{2,1,0:T(8,128)(2,1)S(1)}, bf16[10,8,512]{2,1,0:T(8,128)(2,1)S(1)}, u32[]{:S(2)}, u32[]{:S(2)}) collective-permute-start(bf16[10,8,512]{2,1,0:T(8,128)(2,1)S(1)} %get-tuple-element.49), channel_id=1, source_target_pairs={{0,8},{1,7},{2,10},{3,5},{4,12},{5,3},{6,14},{7,1},{8,0},{9,15},{1... | collective-permute-start | bytes 245768 | tf_op jit(solution)/shard_map/ppermute | solution.py:400
  88.5 4.1 %collective-permute-start.10 = (bf16[10,8,512]{2,1,0:T(8,128)(2,1)S(1)}, bf16[10,8,512]{2,1,0:T(8,128)(2,1)S(1)}, u32[]{:S(2)}, u32[]{:S(2)}) collective-permute-start(bf16[10,8,512]{2,1,0:T(8,128)(2,1)S(1)} %get-tuple-element.50), channel_id=1, source_target_pairs={{0,14},{1,5},{2,12},{3,7},{4,10},{5,1},{6,8},{7,3},{8,6},{9,13},{1... | collective-permute-start | bytes 245768 | tf_op jit(solution)/shard_map/ppermute | solution.py:400
  92.6 0.8 collective-permute-start.11
  93.4 0.4 collective-permute-start.12
  93.8 5.2 %collective-permute-done.9.rest_1_ = bf16[10,8,512]{2,1,0:T(8,128)(2,1)S(1)} collective-permute-done((bf16[10,8,512]{2,1,0:T(8,128)(2,1)S(1)}, bf16[10,8,512]{2,1,0:T(8,128)(2,1)S(1)}, u32[]{:S(2)}, u32[]{:S(2)}) %collective-permute-start.9) | collective-permute-done | bytes 81952 | tf_op jit(solution)/shard_map/ppermute | solution.py:400
  99.0 1.6 %collective-permute-start.13 = (bf16[10,8,512]{2,1,0:T(8,128)(2,1)S(1)}, bf16[10,8,512]{2,1,0:T(8,128)(2,1)S(1)}, u32[]{:S(2)}, u32[]{:S(2)}) collective-permute-start(bf16[10,8,512]{2,1,0:T(8,128)(2,1)S(1)} %get-tuple-element.53), channel_id=1, source_target_pairs={{0,6},{1,11},{2,4},{3,9},{4,2},{5,15},{6,0},{7,13},{8,14},{9,3},{1... | collective-permute-start | bytes 245768 | tf_op jit(solution)/shard_map/ppermute | solution.py:400
  100.6 2.0 %collective-permute-start.14 = (bf16[10,8,512]{2,1,0:T(8,128)(2,1)S(1)}, bf16[10,8,512]{2,1,0:T(8,128)(2,1)S(1)}, u32[]{:S(2)}, u32[]{:S(2)}) collective-permute-start(bf16[10,8,512]{2,1,0:T(8,128)(2,1)S(1)} %get-tuple-element.54), channel_id=1, source_target_pairs={{0,4},{1,9},{2,6},{3,11},{4,0},{5,13},{6,2},{7,15},{8,12},{9,1},{1... | collective-permute-start | bytes 245768 | tf_op jit(solution)/shard_map/ppermute | solution.py:400
  102.7 0.2 collect.6.rest_3_
  102.9 2.1 %attend.3 = (bf16[6,8,512]{2,1,0:T(8,128)(2,1)S(1)}, bf16[6,8,512]{2,1,0:T(8,128)(2,1)S(1)}, bf16[6,8,512]{2,1,0:T(8,128)(2,1)S(1)}, bf16[6,8,512]{2,1,0:T(8,128...) custom-call(f32[32,128]{1,0:T(8,128)S(1)} %bitcast.13, ...), custom_call_target="tpu_custom_call" | custom-call | tf_op jit(solution)/shard_map/attend/pallas_call | solution.py:351
  105.0 1.5 %collective-permute-start.23 = (bf16[6,8,512]{2,1,0:T(8,128)(2,1)S(1)}, bf16[6,8,512]{2,1,0:T(8,128)(2,1)S(1)}, u32[]{:S(2)}, u32[]{:S(2)}) collective-permute-start(bf16[6,8,512]{2,1,0:T(8,128)(2,1)S(1)} %get-tuple-element.67), channel_id=1, source_target_pairs={{0,10},{1,3},{2,8},{3,1},{4,14},{5,7},{6,12},{7,5},{8,2},{9,11},{1... | collective-permute-start | bytes 147464 | tf_op jit(solution)/shard_map/ppermute | solution.py:400
  106.5 0.8 collective-permute-start.24
  107.3 4.4 %collective-permute-start.25 = (bf16[6,8,512]{2,1,0:T(8,128)(2,1)S(1)}, bf16[6,8,512]{2,1,0:T(8,128)(2,1)S(1)}, u32[]{:S(2)}, u32[]{:S(2)}) collective-permute-start(bf16[6,8,512]{2,1,0:T(8,128)(2,1)S(1)} %get-tuple-element.69), channel_id=1, source_target_pairs={{0,14},{1,5},{2,12},{3,7},{4,10},{5,1},{6,8},{7,3},{8,6},{9,13},{1... | collective-permute-start | bytes 147464 | tf_op jit(solution)/shard_map/ppermute | solution.py:400
  111.7 1.0 collective-permute-start.26
  112.9 0.2 collective-permute-done.24.rest_2_
  113.1 3.1 %collective-permute-start.29 = (bf16[6,8,512]{2,1,0:T(8,128)(2,1)S(1)}, bf16[6,8,512]{2,1,0:T(8,128)(2,1)S(1)}, u32[]{:S(2)}, u32[]{:S(2)}) collective-permute-start(bf16[6,8,512]{2,1,0:T(8,128)(2,1)S(1)} %get-tuple-element.73), channel_id=1, source_target_pairs={{0,4},{1,9},{2,6},{3,11},{4,0},{5,13},{6,2},{7,15},{8,12},{9,1},{1... | collective-permute-start | bytes 147464 | tf_op jit(solution)/shard_map/ppermute | solution.py:400
  116.2 0.9 unpack.2.rest_0_
  117.1 0.5 collective-permute-done.26.rest_4_
  117.6 0.6 collective-permute-done.28.rest_6_
  118.2 0.6 collective-permute-done.29.rest_7_
  118.8 0.8 unpack.3
  (27 shorter events, 0.4 us)
Async XLA Ops:
  1.5 13.8 %collective-permute-start = (bf16[121,8,128]{2,1,0:T(8,128)(2,1)S(1)}, bf16[121,8,128]{2,1,0:T(8,128)(2,1)S(1)}, u32[]{:S(2)}, u32[]{:S(2)}) collective-permute-start(bf16[121,8,128]{2,1,0:T(8,128)(2,1)S(1)} %get-tuple-element.40), channel_id=1, source_target_pairs={{0,10},{1,3},{2,8},{3,1},{4,14},{5,7},{6,12},{7,5},{8,2},{9,11},{1... | collective-permute-start | bytes 743432 | tf_op jit(solution)/shard_map/ppermute | solution.py:400
  8.4 30.5 %collective-permute-start.1 = (bf16[121,8,128]{2,1,0:T(8,128)(2,1)S(1)}, bf16[121,8,128]{2,1,0:T(8,128)(2,1)S(1)}, u32[]{:S(2)}, u32[]{:S(2)}) collective-permute-start(bf16[121,8,128]{2,1,0:T(8,128)(2,1)S(1)} %get-tuple-element.41), channel_id=1, source_target_pairs={{0,8},{1,7},{2,10},{3,5},{4,12},{5,3},{6,14},{7,1},{8,0},{9,15},{1... | collective-permute-start | bytes 743432 | tf_op jit(solution)/shard_map/ppermute | solution.py:400
  8.8 31.3 %collective-permute-start.2 = (bf16[121,8,128]{2,1,0:T(8,128)(2,1)S(1)}, bf16[121,8,128]{2,1,0:T(8,128)(2,1)S(1)}, u32[]{:S(2)}, u32[]{:S(2)}) collective-permute-start(bf16[121,8,128]{2,1,0:T(8,128)(2,1)S(1)} %get-tuple-element.42), channel_id=1, source_target_pairs={{0,14},{1,5},{2,12},{3,7},{4,10},{5,1},{6,8},{7,3},{8,6},{9,13},{1... | collective-permute-start | bytes 743432 | tf_op jit(solution)/shard_map/ppermute | solution.py:400
  12.4 27.8 %collective-permute-start.3 = (bf16[121,8,128]{2,1,0:T(8,128)(2,1)S(1)}, bf16[121,8,128]{2,1,0:T(8,128)(2,1)S(1)}, u32[]{:S(2)}, u32[]{:S(2)}) collective-permute-start(bf16[121,8,128]{2,1,0:T(8,128)(2,1)S(1)} %get-tuple-element.43), channel_id=1, source_target_pairs={{0,12},{1,15},{2,14},{3,13},{4,8},{5,11},{6,10},{7,9},{8,4},{9,7},... | collective-permute-start | bytes 743432 | tf_op jit(solution)/shard_map/ppermute | solution.py:400
  12.4 27.7 %collective-permute-start.4 = (bf16[121,8,128]{2,1,0:T(8,128)(2,1)S(1)}, bf16[121,8,128]{2,1,0:T(8,128)(2,1)S(1)}, u32[]{:S(2)}, u32[]{:S(2)}) collective-permute-start(bf16[121,8,128]{2,1,0:T(8,128)(2,1)S(1)} %get-tuple-element.44), channel_id=1, source_target_pairs={{0,2},{1,13},{2,0},{3,15},{4,6},{5,9},{6,4},{7,11},{8,10},{9,5},{1... | collective-permute-start | bytes 743432 | tf_op jit(solution)/shard_map/ppermute | solution.py:400
  15.3 24.8 %collective-permute-start.5 = (bf16[121,8,128]{2,1,0:T(8,128)(2,1)S(1)}, bf16[121,8,128]{2,1,0:T(8,128)(2,1)S(1)}, u32[]{:S(2)}, u32[]{:S(2)}) collective-permute-start(bf16[121,8,128]{2,1,0:T(8,128)(2,1)S(1)} %get-tuple-element.45), channel_id=1, source_target_pairs={{0,6},{1,11},{2,4},{3,9},{4,2},{5,15},{6,0},{7,13},{8,14},{9,3},{1... | collective-permute-start | bytes 743432 | tf_op jit(solution)/shard_map/ppermute | solution.py:400
  38.9 8.9 %collective-permute-start.6 = (bf16[121,8,128]{2,1,0:T(8,128)(2,1)S(1)}, bf16[121,8,128]{2,1,0:T(8,128)(2,1)S(1)}, u32[]{:S(2)}, u32[]{:S(2)}) collective-permute-start(bf16[121,8,128]{2,1,0:T(8,128)(2,1)S(1)} %get-tuple-element.46), channel_id=1, source_target_pairs={{0,4},{1,9},{2,6},{3,11},{4,0},{5,13},{6,2},{7,15},{8,12},{9,1},{1... | collective-permute-start | bytes 743432 | tf_op jit(solution)/shard_map/ppermute | solution.py:400
  48.3 29.3 %collective-permute-start.7 = (bf16[81,64,128]{2,1,0:T(8,128)(2,1)S(1)}, bf16[81,64,128]{2,1,0:T(8,128)(2,1)S(1)}, u32[]{:S(2)}, u32[]{:S(2)}) collective-permute-start(bf16[81,64,128]{2,1,0:T(8,128)(2,1)S(1)} %collect.5.rest_1_), channel_id=1, source_target_pairs={{0,1},{1,0},{2,3},{3,2},{4,5},{5,4},{6,7},{7,6},{8,9},{9,8},{10,11... | collective-permute-start | bytes 3981320 | tf_op jit(solution)/shard_map/ppermute | solution.py:400
  53.2 25.9 %copy-start = (f32[4096]{0:T(1024)S(1)}, f32[4096]{0:T(1024)}, u32[]{:S(2)}) copy-start(f32[4096]{0:T(1024)} %param.11) | copy-start | bytes 49156
  53.2 9.7 %collective-permute-start.15 = (bf16[72,8,128]{2,1,0:T(8,128)(2,1)S(1)}, bf16[72,8,128]{2,1,0:T(8,128)(2,1)S(1)}, u32[]{:S(2)}, u32[]{:S(2)}) collective-permute-start(bf16[72,8,128]{2,1,0:T(8,128)(2,1)S(1)} %get-tuple-element.59), channel_id=1, source_target_pairs={{0,10},{1,3},{2,8},{3,1},{4,14},{5,7},{6,12},{7,5},{8,2},{9,11},{1... | collective-permute-start | bytes 442376 | tf_op jit(solution)/shard_map/ppermute | solution.py:400
  55.1 19.6 %collective-permute-start.16 = (bf16[72,8,128]{2,1,0:T(8,128)(2,1)S(1)}, bf16[72,8,128]{2,1,0:T(8,128)(2,1)S(1)}, u32[]{:S(2)}, u32[]{:S(2)}) collective-permute-start(bf16[72,8,128]{2,1,0:T(8,128)(2,1)S(1)} %get-tuple-element.60), channel_id=1, source_target_pairs={{0,8},{1,7},{2,10},{3,5},{4,12},{5,3},{6,14},{7,1},{8,0},{9,15},{1... | collective-permute-start | bytes 442376 | tf_op jit(solution)/shard_map/ppermute | solution.py:400
  55.6 26.3 %collective-permute-start.17 = (bf16[72,8,128]{2,1,0:T(8,128)(2,1)S(1)}, bf16[72,8,128]{2,1,0:T(8,128)(2,1)S(1)}, u32[]{:S(2)}, u32[]{:S(2)}) collective-permute-start(bf16[72,8,128]{2,1,0:T(8,128)(2,1)S(1)} %get-tuple-element.61), channel_id=1, source_target_pairs={{0,14},{1,5},{2,12},{3,7},{4,10},{5,1},{6,8},{7,3},{8,6},{9,13},{1... | collective-permute-start | bytes 442376 | tf_op jit(solution)/shard_map/ppermute | solution.py:400
  60.6 21.3 %collective-permute-start.18 = (bf16[72,8,128]{2,1,0:T(8,128)(2,1)S(1)}, bf16[72,8,128]{2,1,0:T(8,128)(2,1)S(1)}, u32[]{:S(2)}, u32[]{:S(2)}) collective-permute-start(bf16[72,8,128]{2,1,0:T(8,128)(2,1)S(1)} %get-tuple-element.62), channel_id=1, source_target_pairs={{0,12},{1,15},{2,14},{3,13},{4,8},{5,11},{6,10},{7,9},{8,4},{9,7},... | collective-permute-start | bytes 442376 | tf_op jit(solution)/shard_map/ppermute | solution.py:400
  63.0 18.9 %collective-permute-start.19 = (bf16[72,8,128]{2,1,0:T(8,128)(2,1)S(1)}, bf16[72,8,128]{2,1,0:T(8,128)(2,1)S(1)}, u32[]{:S(2)}, u32[]{:S(2)}) collective-permute-start(bf16[72,8,128]{2,1,0:T(8,128)(2,1)S(1)} %get-tuple-element.63), channel_id=1, source_target_pairs={{0,2},{1,13},{2,0},{3,15},{4,6},{5,9},{6,4},{7,11},{8,10},{9,5},{1... | collective-permute-start | bytes 442376 | tf_op jit(solution)/shard_map/ppermute | solution.py:400
  74.7 7.6 %collective-permute-start.20 = (bf16[72,8,128]{2,1,0:T(8,128)(2,1)S(1)}, bf16[72,8,128]{2,1,0:T(8,128)(2,1)S(1)}, u32[]{:S(2)}, u32[]{:S(2)}) collective-permute-start(bf16[72,8,128]{2,1,0:T(8,128)(2,1)S(1)} %get-tuple-element.64), channel_id=1, source_target_pairs={{0,6},{1,11},{2,4},{3,9},{4,2},{5,15},{6,0},{7,13},{8,14},{9,3},{1... | collective-permute-start | bytes 442376 | tf_op jit(solution)/shard_map/ppermute | solution.py:400
  77.5 7.8 %collective-permute-start.21 = (bf16[72,8,128]{2,1,0:T(8,128)(2,1)S(1)}, bf16[72,8,128]{2,1,0:T(8,128)(2,1)S(1)}, u32[]{:S(2)}, u32[]{:S(2)}) collective-permute-start(bf16[72,8,128]{2,1,0:T(8,128)(2,1)S(1)} %get-tuple-element.65), channel_id=1, source_target_pairs={{0,4},{1,9},{2,6},{3,11},{4,0},{5,13},{6,2},{7,15},{8,12},{9,1},{1... | collective-permute-start | bytes 442376 | tf_op jit(solution)/shard_map/ppermute | solution.py:400
  85.6 15.0 %collective-permute-start.22 = (bf16[48,64,128]{2,1,0:T(8,128)(2,1)S(1)}, bf16[48,64,128]{2,1,0:T(8,128)(2,1)S(1)}, u32[]{:S(2)}, u32[]{:S(2)}) collective-permute-start(bf16[48,64,128]{2,1,0:T(8,128)(2,1)S(1)} %collect.7.rest_4_), channel_id=1, source_target_pairs={{0,1},{1,0},{2,3},{3,2},{4,5},{5,4},{6,7},{7,6},{8,9},{9,8},{10,11... | collective-permute-start | bytes 2359304 | tf_op jit(solution)/shard_map/ppermute | solution.py:400
  85.7 7.7 %collective-permute-start.8 = (bf16[10,8,512]{2,1,0:T(8,128)(2,1)S(1)}, bf16[10,8,512]{2,1,0:T(8,128)(2,1)S(1)}, u32[]{:S(2)}, u32[]{:S(2)}) collective-permute-start(bf16[10,8,512]{2,1,0:T(8,128)(2,1)S(1)} %get-tuple-element.48), channel_id=1, source_target_pairs={{0,10},{1,3},{2,8},{3,1},{4,14},{5,7},{6,12},{7,5},{8,2},{9,11},{1... | collective-permute-start | bytes 245768 | tf_op jit(solution)/shard_map/ppermute | solution.py:400
  87.2 11.8 %collective-permute-start.9 = (bf16[10,8,512]{2,1,0:T(8,128)(2,1)S(1)}, bf16[10,8,512]{2,1,0:T(8,128)(2,1)S(1)}, u32[]{:S(2)}, u32[]{:S(2)}) collective-permute-start(bf16[10,8,512]{2,1,0:T(8,128)(2,1)S(1)} %get-tuple-element.49), channel_id=1, source_target_pairs={{0,8},{1,7},{2,10},{3,5},{4,12},{5,3},{6,14},{7,1},{8,0},{9,15},{1... | collective-permute-start | bytes 245768 | tf_op jit(solution)/shard_map/ppermute | solution.py:400
  88.5 16.4 %collective-permute-start.10 = (bf16[10,8,512]{2,1,0:T(8,128)(2,1)S(1)}, bf16[10,8,512]{2,1,0:T(8,128)(2,1)S(1)}, u32[]{:S(2)}, u32[]{:S(2)}) collective-permute-start(bf16[10,8,512]{2,1,0:T(8,128)(2,1)S(1)} %get-tuple-element.50), channel_id=1, source_target_pairs={{0,14},{1,5},{2,12},{3,7},{4,10},{5,1},{6,8},{7,3},{8,6},{9,13},{1... | collective-permute-start | bytes 245768 | tf_op jit(solution)/shard_map/ppermute | solution.py:400
  92.6 13.9 %collective-permute-start.11 = (bf16[10,8,512]{2,1,0:T(8,128)(2,1)S(1)}, bf16[10,8,512]{2,1,0:T(8,128)(2,1)S(1)}, u32[]{:S(2)}, u32[]{:S(2)}) collective-permute-start(bf16[10,8,512]{2,1,0:T(8,128)(2,1)S(1)} %get-tuple-element.51), channel_id=1, source_target_pairs={{0,12},{1,15},{2,14},{3,13},{4,8},{5,11},{6,10},{7,9},{8,4},{9,7},... | collective-permute-start | bytes 245768 | tf_op jit(solution)/shard_map/ppermute | solution.py:400
  93.4 13.8 %collective-permute-start.12 = (bf16[10,8,512]{2,1,0:T(8,128)(2,1)S(1)}, bf16[10,8,512]{2,1,0:T(8,128)(2,1)S(1)}, u32[]{:S(2)}, u32[]{:S(2)}) collective-permute-start(bf16[10,8,512]{2,1,0:T(8,128)(2,1)S(1)} %get-tuple-element.52), channel_id=1, source_target_pairs={{0,2},{1,13},{2,0},{3,15},{4,6},{5,9},{6,4},{7,11},{8,10},{9,5},{1... | collective-permute-start | bytes 245768 | tf_op jit(solution)/shard_map/ppermute | solution.py:400
  99.0 12.7 %collective-permute-start.13 = (bf16[10,8,512]{2,1,0:T(8,128)(2,1)S(1)}, bf16[10,8,512]{2,1,0:T(8,128)(2,1)S(1)}, u32[]{:S(2)}, u32[]{:S(2)}) collective-permute-start(bf16[10,8,512]{2,1,0:T(8,128)(2,1)S(1)} %get-tuple-element.53), channel_id=1, source_target_pairs={{0,6},{1,11},{2,4},{3,9},{4,2},{5,15},{6,0},{7,13},{8,14},{9,3},{1... | collective-permute-start | bytes 245768 | tf_op jit(solution)/shard_map/ppermute | solution.py:400
  100.6 12.1 %collective-permute-start.14 = (bf16[10,8,512]{2,1,0:T(8,128)(2,1)S(1)}, bf16[10,8,512]{2,1,0:T(8,128)(2,1)S(1)}, u32[]{:S(2)}, u32[]{:S(2)}) collective-permute-start(bf16[10,8,512]{2,1,0:T(8,128)(2,1)S(1)} %get-tuple-element.54), channel_id=1, source_target_pairs={{0,4},{1,9},{2,6},{3,11},{4,0},{5,13},{6,2},{7,15},{8,12},{9,1},{1... | collective-permute-start | bytes 245768 | tf_op jit(solution)/shard_map/ppermute | solution.py:400
  105.0 7.7 %collective-permute-start.23 = (bf16[6,8,512]{2,1,0:T(8,128)(2,1)S(1)}, bf16[6,8,512]{2,1,0:T(8,128)(2,1)S(1)}, u32[]{:S(2)}, u32[]{:S(2)}) collective-permute-start(bf16[6,8,512]{2,1,0:T(8,128)(2,1)S(1)} %get-tuple-element.67), channel_id=1, source_target_pairs={{0,10},{1,3},{2,8},{3,1},{4,14},{5,7},{6,12},{7,5},{8,2},{9,11},{1... | collective-permute-start | bytes 147464 | tf_op jit(solution)/shard_map/ppermute | solution.py:400
  106.5 6.6 %collective-permute-start.24 = (bf16[6,8,512]{2,1,0:T(8,128)(2,1)S(1)}, bf16[6,8,512]{2,1,0:T(8,128)(2,1)S(1)}, u32[]{:S(2)}, u32[]{:S(2)}) collective-permute-start(bf16[6,8,512]{2,1,0:T(8,128)(2,1)S(1)} %get-tuple-element.68), channel_id=1, source_target_pairs={{0,8},{1,7},{2,10},{3,5},{4,12},{5,3},{6,14},{7,1},{8,0},{9,15},{1... | collective-permute-start | bytes 147464 | tf_op jit(solution)/shard_map/ppermute | solution.py:400
  107.3 9.8 %collective-permute-start.25 = (bf16[6,8,512]{2,1,0:T(8,128)(2,1)S(1)}, bf16[6,8,512]{2,1,0:T(8,128)(2,1)S(1)}, u32[]{:S(2)}, u32[]{:S(2)}) collective-permute-start(bf16[6,8,512]{2,1,0:T(8,128)(2,1)S(1)} %get-tuple-element.69), channel_id=1, source_target_pairs={{0,14},{1,5},{2,12},{3,7},{4,10},{5,1},{6,8},{7,3},{8,6},{9,13},{1... | collective-permute-start | bytes 147464 | tf_op jit(solution)/shard_map/ppermute | solution.py:400
  111.7 5.9 %collective-permute-start.26 = (bf16[6,8,512]{2,1,0:T(8,128)(2,1)S(1)}, bf16[6,8,512]{2,1,0:T(8,128)(2,1)S(1)}, u32[]{:S(2)}, u32[]{:S(2)}) collective-permute-start(bf16[6,8,512]{2,1,0:T(8,128)(2,1)S(1)} %get-tuple-element.70), channel_id=1, source_target_pairs={{0,12},{1,15},{2,14},{3,13},{4,8},{5,11},{6,10},{7,9},{8,4},{9,7},... | collective-permute-start | bytes 147464 | tf_op jit(solution)/shard_map/ppermute | solution.py:400
  112.7 4.9 %collective-permute-start.27 = (bf16[6,8,512]{2,1,0:T(8,128)(2,1)S(1)}, bf16[6,8,512]{2,1,0:T(8,128)(2,1)S(1)}, u32[]{:S(2)}, u32[]{:S(2)}) collective-permute-start(bf16[6,8,512]{2,1,0:T(8,128)(2,1)S(1)} %get-tuple-element.71), channel_id=1, source_target_pairs={{0,2},{1,13},{2,0},{3,15},{4,6},{5,9},{6,4},{7,11},{8,10},{9,5},{1... | collective-permute-start | bytes 147464 | tf_op jit(solution)/shard_map/ppermute | solution.py:400
  112.7 5.5 %collective-permute-start.28 = (bf16[6,8,512]{2,1,0:T(8,128)(2,1)S(1)}, bf16[6,8,512]{2,1,0:T(8,128)(2,1)S(1)}, u32[]{:S(2)}, u32[]{:S(2)}) collective-permute-start(bf16[6,8,512]{2,1,0:T(8,128)(2,1)S(1)} %get-tuple-element.72), channel_id=1, source_target_pairs={{0,6},{1,11},{2,4},{3,9},{4,2},{5,15},{6,0},{7,13},{8,14},{9,3},{1... | collective-permute-start | bytes 147464 | tf_op jit(solution)/shard_map/ppermute | solution.py:400
  113.1 5.7 %collective-permute-start.29 = (bf16[6,8,512]{2,1,0:T(8,128)(2,1)S(1)}, bf16[6,8,512]{2,1,0:T(8,128)(2,1)S(1)}, u32[]{:S(2)}, u32[]{:S(2)}) collective-permute-start(bf16[6,8,512]{2,1,0:T(8,128)(2,1)S(1)} %get-tuple-element.73), channel_id=1, source_target_pairs={{0,4},{1,9},{2,6},{3,11},{4,0},{5,13},{6,2},{7,15},{8,12},{9,1},{1... | collective-permute-start | bytes 147464 | tf_op jit(solution)/shard_map/ppermute | solution.py:400
